TPU v7x, 32 devices: a whole 2x2x4 slice. The times are simulated.
32 devices in a mesh: expert: 4 (over y, core), fsdp: 8 (over z, x).
Axes of the slice: x: 2, y: 2, z: 4, core: 2. Of those that a mesh axis runs over, the one named last changes fastest.
Arguments:
- tokens: bfloat16 [8, 1024, 768], P('fsdp', 'expert'), may hold values from -40 to 40
- gain_one: bfloat16 [768], P('fsdp'), may hold values from 0.5 to 1.5
- qkv_weight: bfloat16 [768, 2304], P('fsdp'), may hold values from -0.21875 to 0.21875
- out_weight: bfloat16 [768, 768], P('fsdp'), may hold values from -3.5 to 3.5
- gain_two: bfloat16 [768], P('fsdp'), may hold values from 0.5 to 1.5
- router_weight: bfloat16 [768, 8], P('fsdp'), may hold values from -0.109375 to 0.109375
- const_gate: bfloat16 [768, 4], P('fsdp'), may hold values from -0.21875 to 0.21875
- const_value: bfloat16 [768, 2], P('fsdp'), may hold values from -5 to 5
- expert_gate_up: bfloat16 [4, 768, 4096], P('expert', 'fsdp'), may hold values from -0.21875 to 0.21875
- expert_down: bfloat16 [4, 2048, 768], P('expert', 'fsdp'), may hold values from -0.125 to 0.125
- gate_residual: bfloat16 [8, 1024, 8], P('fsdp', 'expert'), may hold values from -3 to 3
- routes: int32 [8, 1024, 2], P('fsdp', 'expert'), may hold values from 0 to 7, all different within a row; in each aligned block of 256 rows (0 to 255, 256 to 511, ..., all dimensions but the last counted through in order) at most 80 rows name the same one
- cotangent: bfloat16 [8, 1024, 768], P('fsdp', 'expert'), may hold values from -6 to 6
Outputs:
- block_output: bfloat16 [8, 1024, 768], P('fsdp', 'expert')
- grad_tokens: bfloat16 [8, 1024, 768], P('fsdp', 'expert')
- grad_gain_one: float32 [768], P('fsdp')
- grad_qkv: float32 [768, 2304], P('fsdp')
- grad_out: float32 [768, 768], P('fsdp')
- grad_gain_two: float32 [768], P('fsdp')
- grad_router: float32 [768, 8], P('fsdp')
- grad_const_gate: float32 [768, 4], P('fsdp')
- grad_const_value: float32 [768, 2], P('fsdp')
- grad_gate_up: float32 [4, 768, 4096], P('expert', 'fsdp')
- grad_down: float32 [4, 2048, 768], P('expert', 'fsdp')
- grad_gate_residual: bfloat16 [8, 1024, 8], P('fsdp', 'expert')
- stream_rms: float32 [8, 2], P('fsdp')
Inputs may be any that keep to these rules, and one draw needn't show every extreme that they name: In each aligned block of 256 rows (one sequence's positions on one index of expert) no expert is named by more than 80 routes; experts 4 to 7 are the zero, copy and constant experts.
All inputs are finite; a program needn't handle non-finite values.
Results may differ from a plain program's by a relative error of at most 0.024.
Values may be sent and summed in bfloat16 or wider, within the bound.
No kernel may reach another device: no remote copies, remote signals or barrier semaphores. Data moves between devices by JAX's collectives and lax.ppermute only.
A program may use at most 192 MiB of HBM per device.

v0:
```python
import jax
import jax.numpy as jnp
from jax import lax
from jax.sharding import PartitionSpec as P

HEAD = 64
FF = 2048
NCONST = 2
MOST = 80


epsilon = 1e-06
highest = lax.Precision.HIGHEST
masked_score = -1e30


def rms_scale(values):
    return lax.rsqrt(jnp.mean(values * values, axis=-1, keepdims=True) + epsilon)


def rotary(values, positions, direction):
    half_width = values.shape[-1] // 2
    frequency = 10000.0 ** (-jnp.arange(half_width, dtype=jnp.float32) / half_width)
    angles = positions.astype(jnp.float32)[:, None] * frequency[None, :]
    cosine = jnp.cos(angles)[:, None, :]
    sine_part = direction * jnp.sin(angles)[:, None, :]
    former = values[..., :half_width]
    latter = values[..., half_width:]
    return jnp.concatenate(
        [former * cosine - latter * sine_part, latter * cosine + former * sine_part], axis=-1
    )


def local_mixture(
    normed_two, residual_gate, router_full, gate_full, value_full, returned, onehot, expert_count
):
    logits = jnp.dot(normed_two, router_full, precision=highest) + residual_gate
    picked = jnp.sum(onehot * logits[..., None, :], axis=-1)
    gates = jax.nn.softmax(picked, axis=-1)
    mix_logits = jnp.dot(normed_two, gate_full, precision=highest)
    mixing = jax.nn.softmax(mix_logits.reshape(mix_logits.shape[:-1] + (NCONST, 2)), axis=-1)
    const_out = mixing[..., 0:1] * normed_two[..., None, :] + mixing[..., 1:2] * value_full.T
    copy_out = onehot[..., expert_count + 1 : expert_count + 2] * normed_two[..., None, :]
    chosen_const = jnp.einsum(
        "...kc,...cd->...kd", onehot[..., expert_count + 2 :], const_out, precision=highest
    )
    outputs = returned + copy_out + chosen_const
    return jnp.sum(gates[..., None] * outputs, axis=-2)


def take_rows(table, index):
    return table[index]


def norm_input_grad(grad_normed, normed, scale):
    return scale * (grad_normed - normed * jnp.mean(grad_normed * normed, axis=-1, keepdims=True))


def on_device(
    tokens,
    gain_one,
    qkv_weight,
    out_weight,
    gain_two,
    router_weight,
    const_gate,
    const_value,
    expert_gate_up,
    expert_down,
    gate_residual,
    routes,
    cotangent,
):
    full_params = (
        lax.all_gather(gain_one, "fsdp", axis=0, tiled=True),
        lax.all_gather(qkv_weight, "fsdp", axis=0, tiled=True),
        lax.all_gather(out_weight, "fsdp", axis=0, tiled=True),
        lax.all_gather(gain_two, "fsdp", axis=0, tiled=True),
        lax.all_gather(router_weight, "fsdp", axis=0, tiled=True),
        lax.all_gather(const_gate, "fsdp", axis=0, tiled=True),
        lax.all_gather(const_value, "fsdp", axis=0, tiled=True),
        lax.all_gather(expert_gate_up[0], "fsdp", axis=0, tiled=True),
        lax.all_gather(expert_down[0], "fsdp", axis=0, tiled=True),
    )
    (
        gain_one_full,
        qkv_full,
        out_full,
        gain_two_full,
        router_full,
        gate_full,
        value_full,
        gate_up_full,
        down_full,
    ) = full_params
    seq_dev, tok_seq, width = tokens.shape
    groups = lax.axis_size("expert")
    expert_rank = lax.axis_index("expert")
    seq_len = groups * tok_seq
    head_count = width // HEAD
    kind_count = router_full.shape[1]
    most_rows = MOST
    capacity = groups * most_rows
    positions = expert_rank * tok_seq + jnp.arange(tok_seq, dtype=jnp.int32)
    score_scale = HEAD ** (-0.5)
    head_shape = (seq_dev, tok_seq, head_count, HEAD)
    inputs = tokens.astype(jnp.float32)
    scale_one = rms_scale(inputs)
    normed_one = inputs * scale_one
    gain_one_value = gain_one_full.astype(jnp.float32)
    low_one = (normed_one * gain_one_value).astype(jnp.bfloat16)
    projected = jnp.dot(low_one, qkv_full, preferred_element_type=jnp.float32)
    queries = rotary(projected[..., :width].reshape(head_shape), positions, 1.0).astype(
        jnp.bfloat16
    )
    key_rows = rotary(projected[..., width : 2 * width].reshape(head_shape), positions, 1.0).astype(
        jnp.bfloat16
    )
    value_rows = projected[..., 2 * width :].reshape(head_shape).astype(jnp.bfloat16)
    run_max = jnp.full((seq_dev, head_count, tok_seq), masked_score, jnp.float32)
    key_piece = lax.all_gather(key_rows, "expert", axis=1, tiled=True)
    value_piece = lax.all_gather(value_rows, "expert", axis=1, tiled=True)
    piece_rows = key_piece.shape[1]
    scores = (
        jnp.einsum("sqhe,skhe->shqk", queries, key_piece, preferred_element_type=jnp.float32)
        * score_scale
    )
    key_pos = jnp.arange(piece_rows, dtype=jnp.int32)
    visible = positions[:, None] >= key_pos[None, :]
    scores = jnp.where(visible, scores, masked_score)
    new_max = jnp.maximum(run_max, jnp.max(scores, axis=-1))
    weights_now = jnp.where(visible, jnp.exp(scores - new_max[..., None]), 0.0)
    run_total = jnp.sum(weights_now, axis=-1)
    added = jnp.einsum(
        "shqk,skhe->sqhe",
        weights_now.astype(jnp.bfloat16),
        value_piece,
        preferred_element_type=jnp.float32,
    )
    acc_sum = added
    acc_sum, run_max, run_total = (acc_sum, new_max, run_total)
    log_total = run_max + jnp.log(run_total)
    attended = acc_sum / jnp.transpose(run_total, (0, 2, 1))[..., None]
    attended_low = attended.astype(jnp.bfloat16).reshape(seq_dev, tok_seq, width)
    branch = jnp.dot(attended_low, out_full, preferred_element_type=jnp.float32)
    hidden = inputs + branch
    scale_two = rms_scale(hidden)
    normed_two = hidden * scale_two
    gain_two_value = gain_two_full.astype(jnp.float32)
    low_two = (normed_two * gain_two_value).astype(jnp.bfloat16)
    moe_input = low_two.astype(jnp.float32)
    onehot = (routes[..., None] == jnp.arange(kind_count, dtype=jnp.int32)).astype(jnp.float32)
    route_expert = routes.reshape(seq_dev, tok_seq * 2)
    ffn_hot = (route_expert[..., None] == jnp.arange(groups, dtype=jnp.int32)).astype(jnp.int32)
    slot_rank = jnp.sum((jnp.cumsum(ffn_hot, axis=1) - 1) * ffn_hot, axis=-1)
    target = jnp.where(route_expert < groups, route_expert * most_rows + slot_rank, capacity)
    route_index = jnp.arange(tok_seq * 2, dtype=jnp.int32)[None, :]
    sequence_index = jnp.broadcast_to(jnp.arange(seq_dev, dtype=jnp.int32)[:, None], target.shape)
    source_route = (
        jnp.full((seq_dev, capacity + 1), tok_seq * 2, jnp.int32)
        .at[sequence_index, target]
        .set(route_index)[:, :capacity]
    )
    zero_row = jnp.zeros((seq_dev, 1, width), jnp.bfloat16)
    padded_tokens = jnp.concatenate([low_two, zero_row], axis=1)
    send_rows = jax.vmap(take_rows)(padded_tokens, source_route // 2)
    send_rows = send_rows.reshape(seq_dev, groups, most_rows, width)
    received = lax.all_to_all(send_rows, "expert", split_axis=1, concat_axis=1, tiled=True)
    flat_rows = received.reshape(-1, width)
    gate_up = jnp.dot(flat_rows, gate_up_full, preferred_element_type=jnp.float32)
    activation = (jax.nn.silu(gate_up[:, :FF]) * gate_up[:, FF:]).astype(jnp.bfloat16)
    expert_rows = (
        jnp.dot(activation, down_full, preferred_element_type=jnp.float32)
        .astype(jnp.bfloat16)
        .reshape(received.shape)
    )
    back_rows = lax.all_to_all(expert_rows, "expert", split_axis=1, concat_axis=1, tiled=True)
    kept_gate_up = gate_up.reshape(received.shape[:-1] + (2 * FF,))
    flat_returned = jnp.concatenate([back_rows.reshape(seq_dev, capacity, width), zero_row], axis=1)
    route_rows = (
        jax.vmap(take_rows)(flat_returned, target)
        .astype(jnp.float32)
        .reshape(seq_dev, tok_seq, 2, width)
    )
    residual_gate = gate_residual.astype(jnp.float32)

    def mixture(moe_in, residual_in, router_in, gate_in, value_in, routed_in):
        return local_mixture(
            moe_in, residual_in, router_in, gate_in, value_in, routed_in, onehot, groups
        )

    mixture_out, mixture_back = jax.vjp(
        mixture,
        moe_input,
        residual_gate,
        router_full.astype(jnp.float32),
        gate_full.astype(jnp.float32),
        value_full.astype(jnp.float32),
        route_rows,
    )
    outputs = hidden + mixture_out
    hidden_squares = jnp.sum(hidden * hidden, axis=(1, 2))
    output_squares = jnp.sum(outputs * outputs, axis=(1, 2))
    grad_output = cotangent.astype(jnp.float32)
    grad_moe_in, grad_residual, grad_router, grad_const_gate, grad_const_value, grad_routed = (
        mixture_back(grad_output)
    )
    grad_routed_low = grad_routed.astype(jnp.bfloat16).reshape(seq_dev, tok_seq * 2, width)
    padded_grad = jnp.concatenate([grad_routed_low, zero_row], axis=1)
    grad_send = jax.vmap(take_rows)(padded_grad, source_route).reshape(
        seq_dev, groups, most_rows, width
    )
    grad_received = lax.all_to_all(grad_send, "expert", split_axis=1, concat_axis=1, tiled=True)
    back_params = (
        lax.all_gather(gain_one, "fsdp", axis=0, tiled=True),
        lax.all_gather(qkv_weight, "fsdp", axis=0, tiled=True),
        lax.all_gather(out_weight, "fsdp", axis=0, tiled=True),
        lax.all_gather(gain_two, "fsdp", axis=0, tiled=True),
        lax.all_gather(router_weight, "fsdp", axis=0, tiled=True),
        lax.all_gather(const_gate, "fsdp", axis=0, tiled=True),
        lax.all_gather(const_value, "fsdp", axis=0, tiled=True),
        lax.all_gather(expert_gate_up[0], "fsdp", axis=0, tiled=True),
        lax.all_gather(expert_down[0], "fsdp", axis=0, tiled=True),
    )
    qkv_back = back_params[1]
    out_back = back_params[2]
    gate_up_back = back_params[7]
    down_back = back_params[8]
    grad_rows = grad_received.reshape(-1, width)
    gate_up_rows = kept_gate_up.reshape(-1, 2 * FF)
    gate_part = gate_up_rows[:, :FF]
    up_part = gate_up_rows[:, FF:]
    sigmoid_gate = jax.nn.sigmoid(gate_part)
    silu_gate = gate_part * sigmoid_gate
    activation = (silu_gate * up_part).astype(jnp.bfloat16)
    grad_down_w = lax.dot_general(
        activation, grad_rows, (((0,), (0,)), ((), ())), preferred_element_type=jnp.float32
    )
    grad_act = lax.dot_general(
        grad_rows, down_back, (((1,), (1,)), ((), ())), preferred_element_type=jnp.float32
    )
    grad_gate_part = grad_act * up_part * sigmoid_gate * (1.0 + gate_part * (1.0 - sigmoid_gate))
    grad_up_part = grad_act * silu_gate
    grad_gate_up = jnp.concatenate([grad_gate_part, grad_up_part], axis=-1).astype(jnp.bfloat16)
    received_rows = received.reshape(-1, width)
    grad_gate_up_w = lax.dot_general(
        received_rows, grad_gate_up, (((0,), (0,)), ((), ())), preferred_element_type=jnp.float32
    )
    grad_expert_rows = lax.dot_general(
        grad_gate_up, gate_up_back, (((1,), (1,)), ((), ())), preferred_element_type=jnp.float32
    )
    grad_expert_rows = grad_expert_rows.astype(jnp.bfloat16).reshape(grad_received.shape)
    grad_back = lax.all_to_all(grad_expert_rows, "expert", split_axis=1, concat_axis=1, tiled=True)
    padded_back = jnp.concatenate([grad_back.reshape(seq_dev, capacity, width), zero_row], axis=1)
    grad_expert_in = jnp.sum(
        jax.vmap(take_rows)(padded_back, target)
        .astype(jnp.float32)
        .reshape(seq_dev, tok_seq, 2, width),
        axis=2,
    )
    grad_low_two = grad_moe_in + grad_expert_in
    grad_gain_two = jnp.sum(grad_low_two * normed_two, axis=(0, 1))
    grad_hidden = grad_output + norm_input_grad(
        grad_low_two * gain_two_value, normed_two, scale_two
    )
    grad_branch = grad_hidden.astype(jnp.bfloat16)
    grad_out_w = lax.dot_general(
        attended_low, grad_branch, (((0, 1), (0, 1)), ((), ())), preferred_element_type=jnp.float32
    )
    grad_attended = lax.dot_general(
        grad_branch, out_back, (((2,), (1,)), ((), ())), preferred_element_type=jnp.float32
    )
    grad_attended = grad_attended.astype(jnp.bfloat16).reshape(head_shape)
    all_keys, all_values = (
        lax.all_gather(key_rows, "expert", axis=1, tiled=True),
        lax.all_gather(value_rows, "expert", axis=1, tiled=True),
    )
    row_delta = jnp.transpose(
        jnp.sum(grad_attended.astype(jnp.float32) * attended, axis=-1), (0, 2, 1)
    )
    key_blocks = all_keys.reshape(seq_dev, groups, tok_seq, head_count, HEAD).transpose(
        1, 0, 2, 3, 4
    )
    value_blocks = all_values.reshape(seq_dev, groups, tok_seq, head_count, HEAD).transpose(
        1, 0, 2, 3, 4
    )

    def key_block(grad_query, block_in):
        block_keys, block_values, block_index = block_in
        scores = (
            jnp.einsum("sqhe,skhe->shqk", queries, block_keys, preferred_element_type=jnp.float32)
            * score_scale
        )
        key_pos = block_index * tok_seq + jnp.arange(tok_seq, dtype=jnp.int32)
        visible = positions[:, None] >= key_pos[None, :]
        weights_now = jnp.where(visible, jnp.exp(scores - log_total[..., None]), 0.0)
        grad_weights = jnp.einsum(
            "sqhe,skhe->shqk", grad_attended, block_values, preferred_element_type=jnp.float32
        )
        grad_scores = (weights_now * (grad_weights - row_delta[..., None])).astype(jnp.bfloat16)
        grad_query = (
            grad_query
            + jnp.einsum(
                "shqk,skhe->sqhe", grad_scores, block_keys, preferred_element_type=jnp.float32
            )
            * score_scale
        )
        return (grad_query, None)

    grad_query, block_terms = lax.scan(
        key_block,
        jnp.zeros(head_shape, jnp.float32),
        (key_blocks, value_blocks, jnp.arange(groups, dtype=jnp.int32)),
    )
    all_log, all_delta = (
        lax.all_gather(jnp.transpose(log_total, (0, 2, 1)), "expert", axis=1, tiled=True),
        lax.all_gather(jnp.transpose(row_delta, (0, 2, 1)), "expert", axis=1, tiled=True),
    )
    query_piece = lax.all_gather(queries, "expert", axis=1, tiled=True)
    attended_piece = lax.all_gather(grad_attended, "expert", axis=1, tiled=True)
    piece_rows = query_piece.shape[1]
    log_piece = jnp.transpose(all_log, (0, 2, 1))
    delta_piece = jnp.transpose(all_delta, (0, 2, 1))
    scores = (
        jnp.einsum("sqhe,skhe->shqk", query_piece, key_rows, preferred_element_type=jnp.float32)
        * score_scale
    )
    query_pos = jnp.arange(piece_rows, dtype=jnp.int32)
    visible = query_pos[:, None] >= positions[None, :]
    weights_now = jnp.where(visible, jnp.exp(scores - log_piece[..., None]), 0.0)
    grad_weights = jnp.einsum(
        "sqhe,skhe->shqk", attended_piece, value_rows, preferred_element_type=jnp.float32
    )
    grad_scores = (weights_now * (grad_weights - delta_piece[..., None])).astype(jnp.bfloat16)
    key_grad = (
        jnp.einsum("shqk,sqhe->skhe", grad_scores, query_piece, preferred_element_type=jnp.float32)
        * score_scale
    )
    value_grad = jnp.einsum(
        "shqk,sqhe->skhe",
        weights_now.astype(jnp.bfloat16),
        attended_piece,
        preferred_element_type=jnp.float32,
    )
    grad_value_flat = value_grad.reshape(seq_dev, tok_seq, width)
    grad_query_turned = rotary(grad_query, positions, -1.0).reshape(seq_dev, tok_seq, width)
    grad_key_turned = rotary(key_grad, positions, -1.0).reshape(seq_dev, tok_seq, width)
    grad_projected = jnp.concatenate(
        [grad_query_turned, grad_key_turned, grad_value_flat], axis=-1
    ).astype(jnp.bfloat16)
    grad_qkv_w = lax.dot_general(
        low_one, grad_projected, (((0, 1), (0, 1)), ((), ())), preferred_element_type=jnp.float32
    )
    grad_low_one = lax.dot_general(
        grad_projected, qkv_back, (((2,), (1,)), ((), ())), preferred_element_type=jnp.float32
    )
    grad_gain_one = jnp.sum(grad_low_one * normed_one, axis=(0, 1))
    grad_inputs = grad_hidden + norm_input_grad(
        grad_low_one * gain_one_value, normed_one, scale_one
    )
    shards = (
        lax.psum_scatter(
            grad_gain_one.astype(jnp.bfloat16), "fsdp", scatter_dimension=0, tiled=True
        ).astype(jnp.float32),
        lax.psum_scatter(
            grad_qkv_w.astype(jnp.bfloat16), "fsdp", scatter_dimension=0, tiled=True
        ).astype(jnp.float32),
        lax.psum_scatter(
            grad_out_w.astype(jnp.bfloat16), "fsdp", scatter_dimension=0, tiled=True
        ).astype(jnp.float32),
        lax.psum_scatter(
            grad_gain_two.astype(jnp.bfloat16), "fsdp", scatter_dimension=0, tiled=True
        ).astype(jnp.float32),
        lax.psum_scatter(
            grad_router.astype(jnp.bfloat16), "fsdp", scatter_dimension=0, tiled=True
        ).astype(jnp.float32),
        lax.psum_scatter(
            grad_const_gate.astype(jnp.bfloat16), "fsdp", scatter_dimension=0, tiled=True
        ).astype(jnp.float32),
        lax.psum_scatter(
            grad_const_value.astype(jnp.bfloat16), "fsdp", scatter_dimension=0, tiled=True
        ).astype(jnp.float32),
        lax.psum_scatter(
            grad_gate_up_w.astype(jnp.bfloat16), "fsdp", scatter_dimension=0, tiled=True
        ).astype(jnp.float32),
        lax.psum_scatter(
            grad_down_w.astype(jnp.bfloat16), "fsdp", scatter_dimension=0, tiled=True
        ).astype(jnp.float32),
    )
    (
        shard_gain_one,
        shard_qkv,
        shard_out,
        shard_gain_two,
        shard_router,
        shard_const_gate,
        shard_const_value,
        shard_gate_up,
        shard_down,
    ) = shards
    summed = (
        lax.psum(shard_gain_one.astype(jnp.bfloat16), "expert").astype(jnp.float32),
        lax.psum(shard_qkv.astype(jnp.bfloat16), "expert").astype(jnp.float32),
        lax.psum(shard_out.astype(jnp.bfloat16), "expert").astype(jnp.float32),
        lax.psum(shard_gain_two.astype(jnp.bfloat16), "expert").astype(jnp.float32),
        lax.psum(shard_router.astype(jnp.bfloat16), "expert").astype(jnp.float32),
        lax.psum(shard_const_gate.astype(jnp.bfloat16), "expert").astype(jnp.float32),
        lax.psum(shard_const_value.astype(jnp.bfloat16), "expert").astype(jnp.float32),
        lax.psum(hidden_squares.astype(jnp.bfloat16), "expert").astype(jnp.float32),
        lax.psum(output_squares.astype(jnp.bfloat16), "expert").astype(jnp.float32),
    )
    entries_total = seq_len * width
    stream_rms = jnp.stack(
        [jnp.sqrt(summed[7] / entries_total), jnp.sqrt(summed[8] / entries_total)], axis=-1
    )
    return (
        outputs.astype(jnp.bfloat16),
        grad_inputs.astype(jnp.bfloat16),
        summed[0],
        summed[1],
        summed[2],
        summed[3],
        summed[4],
        summed[5],
        summed[6],
        shard_gate_up[None],
        shard_down[None],
        grad_residual.astype(jnp.bfloat16),
        stream_rms,
    )


def solution(mesh):
    return jax.shard_map(
        on_device,
        mesh=mesh,
        in_specs=(
            P("fsdp", "expert", None),
            P("fsdp"),
            P("fsdp", None),
            P("fsdp", None),
            P("fsdp"),
            P("fsdp", None),
            P("fsdp", None),
            P("fsdp", None),
            P("expert", "fsdp", None),
            P("expert", "fsdp", None),
            P("fsdp", "expert", None),
            P("fsdp", "expert", None),
            P("fsdp", "expert", None),
        ),
        out_specs=(
            P("fsdp", "expert", None),
            P("fsdp", "expert", None),
            P("fsdp"),
            P("fsdp", None),
            P("fsdp", None),
            P("fsdp"),
            P("fsdp", None),
            P("fsdp", None),
            P("fsdp", None),
            P("expert", "fsdp", None),
            P("expert", "fsdp", None),
            P("fsdp", "expert", None),
            P("fsdp", None),
        ),
        check_vma=False,
    )
```

profile of v0, /device:TPU:0, one launch (start us, length us, event | category | flops | bytes accessed | tf_op | source)
XLA Modules:
  0.0 1032.0 jit_solution(7990926664601585155)
XLA Ops:
  11.6 23.8 %all-reduce.12 = (bf16[768]{0:T(1024)(128)(2,1)S(1)}, bf16[768]{0:T(1024)(128)(2,1)}) all-reduce(bf16[768]{0:T(1024)(128)(2,1)S(1)} %dynamic-update-slice, bf16[768]{0:T(1024)(128)(2,1)S(1)} %dynamic-update-slice.1), channel_id=1, replica_groups=mesh['expert'=4,'fsdp'=8] {'fsdp'}, use_global_device_ids=true, to_apply=%add.7 | all-reduce | flops 1536 | bytes 6144
  37.5 40.8 %all-gather.15.cloned.1.call-done = bf16[768,2304]{1,0:T(8,128)(2,1)} async-done(((bf16[96,2304]{1,0:T(8,128)(2,1)}), bf16[768,2304]{1,0:T(8,128)(2,1)}) %all-gather.15.cloned.1.call-update) | async-done | bytes 3538960 | tf_op jit(solution)/shard_map/all_gather | solution.py:76
  102.1 26.1 %all-gather.3 = bf16[8,96,8]{1,2,0:T(8,128)(2,1)S(1)} all-gather(bf16[1,96,8]{1,2,0:T(8,128)(2,1)} %bitcast.409), channel_id=1, replica_groups=mesh['expert'=4,'fsdp'=8] {'fsdp'}, dimensions={0}, use_global_device_ids=true | all-gather | bytes 13824 | tf_op jit(solution)/shard_map/all_gather | solution.py:79
  137.8 16.7 %all-gather.4 = bf16[8,96,4]{1,2,0:T(4,128)(2,1)S(1)} all-gather(bf16[1,96,4]{1,2,0:T(4,128)(2,1)} %bitcast.411), channel_id=1, replica_groups=mesh['expert'=4,'fsdp'=8] {'fsdp'}, dimensions={0}, use_global_device_ids=true | all-gather | bytes 6912 | tf_op jit(solution)/shard_map/all_gather | solution.py:80
  157.7 18.3 %all-gather.5 = bf16[8,96,2]{1,2,0:T(2,128)(2,1)S(1)} all-gather(bf16[1,96,2]{1,2,0:T(2,128)(2,1)} %bitcast.412), channel_id=1, replica_groups=mesh['expert'=4,'fsdp'=8] {'fsdp'}, dimensions={0}, use_global_device_ids=true | all-gather | bytes 3456 | tf_op jit(solution)/shard_map/all_gather | solution.py:81
  188.9 7.7 fusion.172
  212.6 9.8 fusion.56
  225.5 7.8 fusion.51
  257.6 35.9 %all-gather.27.cloned.1.call-done = bf16[1,768,4096]{2,1,0:T(8,128)(2,1)} async-done(((bf16[1,96,4096]{2,1,0:T(8,128)(2,1)}), bf16[1,768,4096]{2,1,0:T(8,128)(2,1)}) %all-gather.27.cloned.1.call-update) | async-done | bytes 6291472 | tf_op jit(solution)/shard_map/all_gather | solution.py:82
  293.5 7.5 fusion.30
  300.9 53.4 %all-gather.29.cloned.1.call-done = bf16[1,2048,768]{2,1,0:T(8,128)(2,1)} async-done(((bf16[1,256,768]{2,1,0:T(8,128)(2,1)}), bf16[1,2048,768]{2,1,0:T(8,128)(2,1)}) %all-gather.29.cloned.1.call-update) | async-done | bytes 3145744 | tf_op jit(solution)/shard_map/all_gather | solution.py:83
  385.2 11.4 %multiply_reduce_fusion = (f32[256,2]{1,0:T(8,128)S(1)}, f32[256,768]{1,0:T(8,128)}) fusion(f32[256,768]{1,0:T(8,128)S(1)} %convert_bitcast_fusion, f32[256,2]{1,0:T(8,128)S(1)} %copy-done.23, pred[256,2,2]{1,2,0:T(4,128)(4,1)} %copy.222, f32[2,768]{1,0:T(2,128)S(1)} %bitcast.407, f32[256,2]{1,0:T(8,128)} %copy-done.30, f32[256,2]{1,0:T(8,128)} %copy-done.29, ...), kind=kOutput, calls=%fused_computation.81 | convolution fusion | flops 13172224 | bytes 3949568 | tf_op jit(solution)/shard_map/jvp(...kc,...cd->...kd)/dot_general | solution.py:44
  423.6 29.2 %while.11 = (s32[]{:T(128)}, f32[1,256,12,64]{1,3,2,0:T(8,128)}, bf16[4,1,256,12,64]{2,4,3,1,0:T(8,128)(2,1)}, s32[4]{0:T(128)S(1)}, bf16[1,256,12,64]{1,3,2,0:T...) while((s32[]{:T(128)}, f32[1,256,12,64]{1,3,2,0:T(8,128)}, ...), condition=%wide.region_26.27_spmd.clone, body=%wide.region_25.26_spmd.clone.sunk | while | flops 307364352 | bytes 10000039 | solution.py:310
  452.9 11.0 %fusion.80 = f32[1,256,12,64]{1,3,2,0:T(8,128)S(1)} fusion(f32[12,1024,256]{2,1,0:T(8,128)} %fusion.51, f32[12,1024]{1,0:T(8,128)} %bitcast.403, f32[12,1024]{1,0:T(8,128)} %bitcast.401, pred[1024,256]{1,0:T(8,128)(4,1)} %iota_compare_fusion, bf16[256,12,64]{0,2,1:T(8,128)(2,1)} %bitcast.383, bf16[1,1024,12,64]{1,3,2,0:T(8,128)(2,1)} %all-gather.25.cloned.1.call-done, ...), kind=kOutput, calls=%fused_computation.98 | convolution fusion | flops 824377344 | bytes 17268736 | tf_op jit(solution)/shard_map/shqk,sqhe->skhe/dot_general | solution.py:336
  484.4 30.5 %reduce-scatter.16.cloned.1.call-done = bf16[96,768]{1,0:T(8,128)(2,1)} async-done(((bf16[768,768]{1,0:T(8,128)(2,1)}), bf16[96,768]{1,0:T(8,128)(2,1)}) %reduce-scatter.16.cloned.1.call-update) | async-done | bytes 147472 | tf_op jit(solution)/shard_map/reduce_scatter | solution.py:368
  514.9 81.7 %reduce-scatter.14.cloned.1.call-done = bf16[96,2304]{1,0:T(8,128)(2,1)} async-done(((bf16[768,2304]{1,0:T(8,128)(2,1)}), bf16[96,2304]{1,0:T(8,128)(2,1)}) %reduce-scatter.14.cloned.1.call-update) | async-done | bytes 442384 | tf_op jit(solution)/shard_map/reduce_scatter | solution.py:365
  596.7 8.0 convolution_convert_fusion
  605.3 55.8 %reduce-scatter.26.cloned.1.call-done = bf16[96,2]{1,0:T(8,128)(2,1)} async-done(((bf16[768,2]{1,0:T(8,128)(2,1)}), bf16[96,2]{1,0:T(8,128)(2,1)}) %reduce-scatter.26.cloned.1.call-update) | async-done | bytes 400
  661.9 63.1 %reduce-scatter.24.cloned.1.call-done = bf16[96,4]{1,0:T(8,128)(2,1)} async-done(((bf16[768,4]{1,0:T(8,128)(2,1)}), bf16[96,4]{1,0:T(8,128)(2,1)}) %reduce-scatter.24.cloned.1.call-update) | async-done | bytes 784
  726.6 62.4 %reduce-scatter.22.cloned.1.call-done = bf16[96,8]{1,0:T(8,128)(2,1)} async-done(((bf16[768,8]{1,0:T(8,128)(2,1)}), bf16[96,8]{1,0:T(8,128)(2,1)}) %reduce-scatter.22.cloned.1.call-update) | async-done | bytes 1552
  793.2 19.8 %all-reduce.11 = (bf16[768]{0:T(1024)(128)(2,1)S(1)}, bf16[768]{0:T(1024)(128)(2,1)S(1)}) all-reduce(bf16[768]{0:T(1024)(128)(2,1)S(1)} %get-tuple-element.268, bf16[768]{0:T(1024)(128)(2,1)S(1)} %copy-done.54), channel_id=5, replica_groups=mesh['expert'=4,'fsdp'=8] {'fsdp'}, use_global_device_ids=true, to_apply=%region_29.30.clone | all-reduce | flops 1536 | bytes 6144
  825.6 40.4 %reduce-scatter.20.cloned.1.call-done = bf16[256,768]{1,0:T(8,128)(2,1)} async-done(((bf16[2048,768]{1,0:T(8,128)(2,1)}), bf16[256,768]{1,0:T(8,128)(2,1)}) %reduce-scatter.20.cloned.1.call-update) | async-done | bytes 393232 | tf_op jit(solution)/shard_map/reduce_scatter | solution.py:386
  868.0 33.1 %all-reduce.17.cloned.1.call-done = (bf16[96,2304]{1,0:T(8,128)(2,1)}, bf16[96,768]{1,0:T(8,128)(2,1)}) async-done(((bf16[96,2304]{1,0:T(8,128)(2,1)}, bf16[96,768]{1,0:T(8,128)(2,1)}), (bf16[96,2304]{1,0:T(8,128)(2,1)}, bf16[96,768]{1,0:T(8,128)(2,1)})) %all-reduce.17.cloned.1.call-update) | async-done | bytes 589840 | tf_op jit(solution)/shard_map/psum | solution.py:403
  904.8 117.8 %reduce-scatter.18.cloned.1.call-done = bf16[96,4096]{1,0:T(8,128)(2,1)} async-done(((bf16[768,4096]{1,0:T(8,128)(2,1)}), bf16[96,4096]{1,0:T(8,128)(2,1)}) %reduce-scatter.18.cloned.1.call-update) | async-done | bytes 786448 | tf_op jit(solution)/shard_map/reduce_scatter | solution.py:383
  (354 shorter events, 228.5 us)
Async XLA Ops:
  7.2 71.1 %all-gather.15.cloned.1.call-start = ((), (), s32[]{:S(2)}) async-start(), calls=%async_computation.11 | async-start | bytes 3981312 | tf_op jit(solution)/shard_map/all_gather | solution.py:76
  7.9 168.2 %all-gather.19.cloned.1.call-start = ((), (), s32[]{:S(2)}) async-start(), calls=%async_computation.13 | async-start | bytes 1966080 | tf_op jit(solution)/shard_map/all_gather | solution.py:121
  35.4 46.1 %copy-start.40 = (f32[768]{0:T(1024)}, f32[768]{0:T(1024)S(1)}, u32[]{:S(2)}) copy-start(f32[768]{0:T(1024)S(1)} %convert_element_type.291) | copy-start | bytes 9220
  36.6 44.9 %copy-start.52 = (f32[256]{0:T(256)}, f32[256]{0:T(256)S(1)}, u32[]{:S(2)}) copy-start(f32[256]{0:T(256)S(1)} %add_rsqrt_fusion.1) | copy-start | bytes 3076
  89.4 99.5 %all-gather.17.cloned.1.call-start = ((), (), s32[]{:S(2)}) async-start(), calls=%async_computation.12 | async-start | bytes 1966080 | tf_op jit(solution)/shard_map/all_gather | solution.py:122
  92.2 104.4 %all-gather.21.cloned.1.call-start = ((), (), s32[]{:S(2)}) async-start(), calls=%async_computation.14 | async-start | bytes 1327104 | tf_op jit(solution)/shard_map/all_gather | solution.py:77
  92.8 132.7 %all-gather.23.cloned.1.call-start = ((), (), s32[]{:S(2)}) async-start(), calls=%async_computation.15 | async-start | bytes 1966080 | tf_op jit(solution)/shard_map/all_gather | solution.py:319
  93.7 199.8 %all-gather.27.cloned.1.call-start = ((), (), s32[]{:S(2)}) async-start(), calls=%async_computation.21 | async-start | bytes 7077888 | tf_op jit(solution)/shard_map/all_gather | solution.py:82
  94.3 260.1 %all-gather.29.cloned.1.call-start = ((), (), s32[]{:S(2)}) async-start(), calls=%async_computation.22 | async-start | bytes 3538944 | tf_op jit(solution)/shard_map/all_gather | solution.py:83
  128.3 71.6 %copy-start.31 = (bf16[768,8]{0,1:T(8,128)(2,1)}, bf16[768,8]{0,1:T(8,128)(2,1)S(1)}, u32[]{:S(2)}) copy-start(bf16[768,8]{0,1:T(8,128)(2,1)S(1)} %reshape.1164) | copy-start | bytes 36868
  154.6 45.1 %copy-start.38 = (bf16[768,4]{0,1:T(4,128)(2,1)}, bf16[768,4]{0,1:T(4,128)(2,1)S(1)}, u32[]{:S(2)}) copy-start(bf16[768,4]{0,1:T(4,128)(2,1)S(1)} %reshape.1166) | copy-start | bytes 18436
  207.6 46.1 %all-to-all-start = ((bf16[1,4,80,768]{3,2,0,1:T(8,128)(2,1)}), bf16[1,4,80,768]{3,2,0,1:T(8,128)(2,1)}, u32[]{:S(2)}, u32[]{:S(2)}) async-start(bf16[1,4,80,768]{3,2,0,1:T(8,128)(2,1)} %bitcast.31), calls=%async_computation | async-start | bytes 983040 | tf_op jit(solution)/shard_map/all_to_all | solution.py:168
  253.6 100.7 %all-to-all-start.2 = ((bf16[1,4,80,768]{3,2,0,1:T(8,128)(2,1)}), bf16[1,4,80,768]{3,2,0,1:T(8,128)(2,1)S(1)}, u32[]{:S(2)}, u32[]{:S(2)}) async-start(bf16[1,4,80,768]{3,2,0,1:T(8,128)(2,1)} %bitcast.373), calls=%async_computation.2 | async-start | bytes 983040 | tf_op jit(solution)/shard_map/all_to_all | solution.py:213
  363.6 11.9 %all-to-all-start.1 = ((bf16[1,4,80,768]{3,2,0,1:T(8,128)(2,1)}), bf16[1,4,80,768]{3,2,0,1:T(8,128)(2,1)S(1)}, u32[]{:S(2)}, u32[]{:S(2)}) async-start(bf16[1,4,80,768]{3,2,0,1:T(8,128)(2,1)} %bitcast.36), calls=%async_computation.1 | async-start | bytes 983040 | tf_op jit(solution)/shard_map/all_to_all | solution.py:177
  375.5 21.3 %all-to-all-start.3 = ((bf16[1,4,80,768]{3,2,0,1:T(8,128)(2,1)}), bf16[1,4,80,768]{3,2,0,1:T(8,128)(2,1)S(1)}, u32[]{:S(2)}, u32[]{:S(2)}) async-start(bf16[1,4,80,768]{3,2,0,1:T(8,128)(2,1)} %bitcast.59), calls=%async_computation.3 | async-start | bytes 983040 | tf_op jit(solution)/shard_map/all_to_all | solution.py:253
  379.0 73.9 %all-gather.25.cloned.1.call-start = ((), (), s32[]{:S(2)}) async-start(), calls=%async_computation.16 | async-start | bytes 1966080 | tf_op jit(solution)/shard_map/all_gather | solution.py:320
  414.6 100.3 %reduce-scatter.16.cloned.1.call-start = ((), (), s32[]{:S(2)}) async-start(), calls=%async_computation.18 | async-start | bytes 1327104 | tf_op jit(solution)/shard_map/reduce_scatter | solution.py:368
  452.8 143.8 %reduce-scatter.14.cloned.1.call-start = ((), (), s32[]{:S(2)}) async-start(), calls=%async_computation.17 | async-start | bytes 3981312 | tf_op jit(solution)/shard_map/reduce_scatter | solution.py:365
  475.5 185.6 %reduce-scatter.26.cloned.1.call-start = ((), (), s32[]{:S(2)}) async-start(), calls=%async_computation.25 | async-start | bytes 221184
  477.0 248.0 %reduce-scatter.24.cloned.1.call-start = ((), (), s32[]{:S(2)}) async-start(), calls=%async_computation.24 | async-start | bytes 221184
  478.2 310.8 %reduce-scatter.22.cloned.1.call-start = ((), (), s32[]{:S(2)}) async-start(), calls=%async_computation.23 | async-start | bytes 221184
  479.4 386.7 %reduce-scatter.20.cloned.1.call-start = ((), (), s32[]{:S(2)}) async-start(), calls=%async_computation.20 | async-start | bytes 3538944 | tf_op jit(solution)/shard_map/reduce_scatter | solution.py:386
  484.4 416.8 %all-reduce.17.cloned.1.call-start = ((), (), s32[]{:S(2)}) async-start(), calls=%async_computation.26 | async-start | bytes 1179648 | tf_op jit(solution)/shard_map/psum | solution.py:403
  596.6 426.0 %reduce-scatter.18.cloned.1.call-start = ((), (), s32[]{:S(2)}) async-start(), calls=%async_computation.19 | async-start | bytes 7077888 | tf_op jit(solution)/shard_map/reduce_scatter | solution.py:383
  (59 other events, 437.3 us)
Sparse Core Ops, SparseCore 0:
  10.2 68.0 all-gather.14
  89.5 18.3 all-gather.18
  109.5 19.7 all-gather.16
  131.4 40.9 all-gather.20
  173.7 18.5 all-gather.22
  194.4 99.0 all-gather.26
  295.7 58.6 all-gather.28
  414.8 18.9 all-gather.24
  452.9 61.9 reduce-scatter.15
  518.4 78.1 reduce-scatter.13
  600.4 60.6 reduce-scatter.25
  664.8 60.1 reduce-scatter.23
  728.9 60.1 reduce-scatter.21
  792.5 73.5 reduce-scatter.19
  868.4 32.6 all-reduce.16
  904.6 117.9 reduce-scatter.17
where the time goes:
time: 1040 us; the launch traced here: 1030 us
  waiting for transfers between devices  619 us (60%)
  matrix products  136 us (13%)
  blocking collectives  125 us (12%)
  local copies, waits for them, and re-layouts  71.9 us (7%)
  other arithmetic  42.6 us (4%)
  between operations  18.1 us (2%)
  starting transfers between devices  16.2 us (2%)
    unnamed x19, waiting for transfers between devices  184 us
    reduce_scatter x1, waiting for transfers between devices, on_device(): lax.psum_scatter(grad_gate_up_w.astype(jnp.bfloat16), 'fsdp', scatter_dim...  118 us
    reduce_scatter x1, waiting for transfers between devices, on_device(): lax.psum_scatter(grad_qkv_w.astype(jnp.bfloat16), 'fsdp', scatter_dimensi...  81.7 us
    all_gather x1, waiting for transfers between devices, on_device(): lax.all_gather(expert_down[0], 'fsdp', axis=0, tiled=True)  53.4 us
    unnamed x2, blocking collectives  43.6 us
    all_gather x1, waiting for transfers between devices, on_device(): lax.all_gather(qkv_weight, 'fsdp', axis=0, tiled=True)  40.8 us
    reduce_scatter x1, waiting for transfers between devices, on_device(): lax.psum_scatter(grad_down_w.astype(jnp.bfloat16), 'fsdp', scatter_dimens...  40.4 us
    all_gather x1, waiting for transfers between devices, on_device(): lax.all_gather(expert_gate_up[0], 'fsdp', axis=0, tiled=True)  35.9 us
  transfers between devices with their start and end apart: 20, of which 12 were waited for; matrix products, arithmetic and copies ran while one was open for 20% of the time, Pallas kernels for 0%

commit v1 on v0

v1 whole, which is shorter than its diff:
```python
import functools

import jax
import jax.numpy as jnp
from jax import lax
from jax.experimental import pallas as pl
from jax.experimental.pallas import tpu as pltpu
from jax.sharding import PartitionSpec as P

HEAD = 64
FF = 2048
NCONST = 2
MOST = 80
PAIR = 2 * HEAD
SMALL = 128

epsilon = 1e-06
masked_score = -1e30
BF = jnp.bfloat16
F32 = jnp.float32


def mm(a, b):
    return jnp.dot(a, b, preferred_element_type=F32)


def mm_nt(a, b):
    return lax.dot_general(a, b, (((1,), (1,)), ((), ())), preferred_element_type=F32)


def mm_tn(a, b):
    return lax.dot_general(a, b, (((0,), (0,)), ((), ())), preferred_element_type=F32)


def split_low(values):
    high = values.astype(BF)
    return high, (values - high.astype(F32)).astype(BF)


def lanes(shape):
    return lax.broadcasted_iota(jnp.int32, shape, len(shape) - 1)


def rows_of(shape):
    return lax.broadcasted_iota(jnp.int32, shape, 0)


def rms_scale(values):
    return lax.rsqrt(jnp.mean(values * values, axis=-1, keepdims=True) + epsilon)


def turned(values, cosine, sine):
    lane = lanes(values.shape) % HEAD
    swapped = jnp.where(
        lane < HEAD // 2,
        pltpu.roll(values, PAIR - HEAD // 2, 1),
        pltpu.roll(values, HEAD // 2, 1),
    )
    return values * cosine + swapped * sine


def call(kernel, outs, args, grid=(), in_specs=None, out_specs=None, scratch=(), scalars=1, name=None):
    whole = pl.BlockSpec(memory_space=pltpu.VMEM)
    multi = isinstance(outs, (tuple, list))
    if in_specs is None:
        in_specs = [whole] * (len(args) - scalars)
    if out_specs is None:
        out_specs = [whole] * len(outs) if multi else whole
    return pl.pallas_call(
        kernel,
        out_shape=outs,
        grid_spec=pltpu.PrefetchScalarGridSpec(
            num_scalar_prefetch=scalars,
            grid=grid,
            in_specs=in_specs,
            out_specs=out_specs,
            scratch_shapes=list(scratch),
        ),
        compiler_params=pltpu.CompilerParams(vmem_limit_bytes=56 * 1024 * 1024),
        name=name,
    )(*args)


def shaped(shape, dtype):
    return jax.ShapeDtypeStruct(shape, dtype)


def swap(values, axis, bits):
    size = lax.axis_size(axis)
    return lax.ppermute(values, axis, [(i, i ^ bits) for i in range(size)])


def along(values, pairs):
    return lax.ppermute(
        values, "fsdp", [(2 * i + b, 2 * j + b) for i, j in pairs for b in (0, 1)]
    )


def after(values, *others):
    return lax.optimization_barrier((values,) + tuple(others))[0]


def major_gather(values):
    major = lax.axis_size("fsdp") // 2
    if major != 4:
        groups = [[2 * i + b for i in range(major)] for b in (0, 1)]
        return lax.all_gather(values, "fsdp", axis=0, tiled=True, axis_index_groups=groups)
    mine = lax.axis_index("fsdp") // 2
    far = along(values, [(0, 2), (2, 0), (1, 3), (3, 1)])
    middle = along(values, [(1, 2), (2, 1)])
    near = along(values, [(0, 1), (1, 0), (2, 3), (3, 2)])
    onward = along(far, [(2, 3), (1, 0)])
    inner = jnp.logical_or(mine == 1, mine == 2).astype(jnp.int32)
    scalars = jnp.stack([mine, mine ^ 1, mine ^ 2, mine ^ 3, inner]).astype(jnp.int32)
    rows = values.shape[0]

    def kernel(where, own, near_ref, far_ref, middle_ref, onward_ref, out):
        def put(slot, ref):
            out[pl.ds(pl.multiple_of(where[slot] * rows, rows), rows), :] = ref[...]

        put(0, own)
        put(1, near_ref)
        put(2, far_ref)

        @pl.when(where[4] == 1)
        def _():
            put(3, middle_ref)

        @pl.when(where[4] == 0)
        def _():
            put(3, onward_ref)

    return call(
        kernel,
        shaped((4 * rows,) + values.shape[1:], values.dtype),
        (scalars, values, near, far, middle, onward),
        name="place_parts",
    )


def major_scatter_sum(full):
    major = lax.axis_size("fsdp") // 2
    rows = full.shape[0] // major
    if major != 4:
        groups = [[2 * i + b for i in range(major)] for b in (0, 1)]
        return lax.psum_scatter(
            full, "fsdp", scatter_dimension=0, tiled=True, axis_index_groups=groups
        ).astype(F32)
    mine = lax.axis_index("fsdp") // 2

    def block(bits):
        return lax.dynamic_slice_in_dim(full, (mine ^ bits) * rows, rows, 0)

    third = block(3)
    first = along(third, [(0, 1), (3, 2)])
    far = along(block(2) + first, [(0, 2), (2, 0), (1, 3), (3, 1)])
    middle = along(third, [(1, 2), (2, 1)])
    near = along(block(1), [(0, 1), (1, 0), (2, 3), (3, 2)])
    return (
        block(0).astype(F32) + near.astype(F32) + far.astype(F32) + middle.astype(F32)
    )


def shared_gather(qkv, out, small):
    parts = lax.axis_size("fsdp")
    if parts != 8:
        return tuple(
            lax.all_gather(v, "fsdp", axis=0, tiled=True) for v in (qkv, out, small)
        ), None
    core = lax.axis_index("expert") % 2
    me = lax.axis_index("fsdp")
    half_qkv, half_out = qkv.shape[1] // 2, out.shape[1] // 2
    mine = jnp.concatenate(
        [
            lax.dynamic_slice_in_dim(qkv, core * half_qkv, half_qkv, 1),
            lax.dynamic_slice_in_dim(out, core * half_out, half_out, 1),
            small,
        ],
        axis=1,
    )
    major = [mine] + [swap(mine, "fsdp", 2 * j) for j in (1, 2, 3)]
    minor = [swap(v, "fsdp", 1) for v in major]
    slots = [2 * j for j in range(4)] + [2 * j + 1 for j in range(4)]
    own = jnp.concatenate(major + minor, axis=0)
    other = swap(own, "expert", 1)
    scalars = jnp.stack([me ^ s for s in slots] + [core]).astype(jnp.int32)
    rows = qkv.shape[0]

    def kernel(where, own_ref, other_ref, qkv_ref, out_ref, small_ref):
        first = where[8] == 0
        for index in range(8):
            source = pl.ds(index * rows, rows)
            target = pl.ds(pl.multiple_of(where[index] * rows, rows), rows)
            a, b = own_ref[source, :], other_ref[source, :]
            left = jnp.where(first, a, b)
            right = jnp.where(first, b, a)
            qkv_ref[target, :half_qkv] = left[:, :half_qkv]
            qkv_ref[target, half_qkv:] = right[:, :half_qkv]
            out_ref[target, :half_out] = left[:, half_qkv : half_qkv + half_out]
            out_ref[target, half_out:] = right[:, half_qkv : half_qkv + half_out]
            small_ref[target, :] = a[:, half_qkv + half_out :]

    full = call(
        kernel,
        [
            shaped((8 * rows, qkv.shape[1]), BF),
            shaped((8 * rows, out.shape[1]), BF),
            shaped((8 * rows, SMALL), BF),
        ],
        (scalars, own, other),
        name="place_shared",
    )
    return tuple(full), tuple(major)


def shared_scatter_sum(left, right):
    parts = lax.axis_size("fsdp")
    if parts != 8 or lax.axis_size("expert") != 4:
        full = jnp.concatenate([left, right], axis=1)
        shard = lax.psum_scatter(full, "fsdp", scatter_dimension=0, tiled=True)
        return lax.psum(shard, "expert").astype(F32)
    core = lax.axis_index("expert") % 2
    me = lax.axis_index("fsdp")
    minor, major = me % 2, me // 2
    first = core == 0
    away = jnp.where(first, right, left)
    kept = jnp.where(first, left, right)
    columns = left.shape[1]
    rows = left.shape[0] // 8
    both = (kept.astype(F32) + swap(away, "expert", 1).astype(F32)).astype(BF)
    both = both.reshape(4, 2, rows, columns)
    away = lax.dynamic_index_in_dim(both, 1 - minor, 1, False)
    kept = lax.dynamic_index_in_dim(both, minor, 1, False)
    both = (kept.astype(F32) + swap(away, "fsdp", 1).astype(F32)).astype(BF)
    total = lax.dynamic_index_in_dim(both, major, 0, False).astype(F32)
    for j in (1, 2, 3):
        total += swap(
            lax.dynamic_index_in_dim(both, major ^ j, 0, False), "fsdp", 2 * j
        ).astype(F32)
    total = total.astype(BF)
    total = (total.astype(F32) + swap(total, "expert", 2).astype(F32)).astype(BF)
    other = swap(total, "expert", 1)
    return jnp.concatenate(
        [jnp.where(first, total, other), jnp.where(first, other, total)], axis=1
    ).astype(F32)


def sequence_gather(values):
    size = lax.axis_size("expert")
    me = lax.axis_index("expert")
    if size != 4:
        return lax.all_gather(values, "expert", axis=0, tiled=True), list(range(size))
    pair = jnp.concatenate([values, swap(values, "expert", 2)], axis=0)
    return jnp.concatenate([pair, swap(pair, "expert", 1)], axis=0), [
        me,
        me ^ 2,
        me ^ 1,
        me ^ 3,
    ]


def sequence_scatter_sum(full, rows):
    size = lax.axis_size("expert")
    me = lax.axis_index("expert")
    if size != 4:
        return lax.psum_scatter(full, "expert", scatter_dimension=0, tiled=True).astype(F32)

    def block(bits):
        return lax.dynamic_slice_in_dim(full, (me ^ bits) * rows, rows, 0)

    away = jnp.concatenate([block(1), block(3)], axis=0)
    kept = jnp.concatenate([block(0), block(2)], axis=0)
    both = kept.astype(F32) + swap(away, "expert", 1).astype(F32)
    return both[:rows] + swap(both[rows:].astype(BF), "expert", 2).astype(F32)


def project_kernel(where, tok, weight, small_t, cosine, sine, q, k, v, normed, *, slots, gain_at):
    step = pl.program_id(0)
    rank = where[step]
    own = where[slots]
    width = tok.shape[1]

    @pl.when(rank > own)
    def _():
        k[...] = jnp.zeros_like(k)
        v[...] = jnp.zeros_like(v)
        normed[...] = jnp.zeros_like(normed)

    @pl.when(rank <= own)
    def _():
        x = tok[...].astype(F32)
        low = ((x * rms_scale(x)) * small_t[gain_at : gain_at + 1, :]).astype(BF)
        normed[...] = low
        cos, sin = cosine[...], sine[...]
        keys = mm(low, weight[:, width : 2 * width])
        for at in range(0, width, PAIR):
            k[:, at : at + PAIR] = turned(keys[:, at : at + PAIR], cos, sin).astype(BF)
        v[...] = mm(low, weight[:, 2 * width :]).astype(BF)

        @pl.when(rank == own)
        def _():
            queries = mm(low, weight[:, :width])
            for at in range(0, width, PAIR):
                q[:, at : at + PAIR] = turned(queries[:, at : at + PAIR], cos, sin).astype(BF)


def stacked_heads(values, scale=None):
    lane = lanes(values.shape)
    if scale is not None:
        values = values * jnp.asarray(scale, values.dtype)
    zero = jnp.zeros_like(values)
    return jnp.concatenate(
        [jnp.where(lane < HEAD, values, zero), jnp.where(lane < HEAD, zero, values)], axis=0
    )


def visible_keys(own, keys, count):
    key = lax.broadcasted_iota(jnp.int32, (keys, 2 * count), 0)
    query = lax.broadcasted_iota(jnp.int32, (keys, 2 * count), 1) % count
    return key <= query + own * count


def attend_kernel(where, q, k, v, attended, log_total, *, slots):
    own = where[slots]
    count, keys = q.shape[0], k.shape[0]
    query = stacked_heads(q[...], HEAD ** (-0.5))
    scores = mm_nt(k[...], query)
    scores = jnp.where(visible_keys(own, keys, count), scores, masked_score)
    top = jnp.max(scores, axis=0, keepdims=True)
    weights = jnp.exp(scores - top)
    total = jnp.sum(weights, axis=0, keepdims=True)
    log_total[...] = jnp.broadcast_to(top + jnp.log(total), (8, 2 * count))[None]
    weights = (weights * (1.0 / total)).astype(BF)
    both = mm_tn(weights, v[...])
    lane = lanes((count, PAIR))
    attended[...] = jnp.where(lane < HEAD, both[:count], both[count:]).astype(BF)


def attend_back_kernel(where, q, k, v, grad_att, log_total, cosine, sine, cos_own, sin_own, dq, dk, dv, *, slots):
    own = where[slots]
    count, keys = q.shape[0], k.shape[0]
    query = stacked_heads(q[...], HEAD ** (-0.5))
    grad_rows = stacked_heads(grad_att[...])
    key_rows = k[...]
    scores = mm_nt(key_rows, query)
    weights = jnp.where(
        visible_keys(own, keys, count), jnp.exp(scores - log_total[0, :1, :]), 0.0
    )
    grad_weights = mm_nt(v[...], grad_rows)
    delta = jnp.sum(weights * grad_weights, axis=0, keepdims=True)
    grad_scores = (weights * (grad_weights - delta)).astype(BF)
    dv[...] = mm(weights.astype(BF), grad_rows).astype(BF)
    dk[...] = turned(mm(grad_scores, query), cosine[...], -sine[...]).astype(BF)
    both = mm_tn(grad_scores, key_rows)
    lane = lanes((count, PAIR))
    grad_query = jnp.where(lane < HEAD, both[:count], both[count:]) * HEAD ** (-0.5)
    dq[...] = turned(grad_query, cos_own[...], -sin_own[...]).astype(BF)


def routing(routes, resid, logits, groups):
    count = routes.shape[0]
    lane = lanes((count, SMALL))
    kind = lanes(resid.shape)
    hot, picked = [], []
    for choice in range(2):
        route = routes[:, choice : choice + 1]
        hot.append(lane == route)
        picked.append(
            jnp.sum(jnp.where(hot[choice], logits, 0.0), axis=-1, keepdims=True)
            + jnp.sum(jnp.where(kind == route, resid, 0.0), axis=-1, keepdims=True)
        )
    top = jnp.maximum(picked[0], picked[1])
    first, second = jnp.exp(picked[0] - top), jnp.exp(picked[1] - top)
    gates = [first / (first + second), second / (first + second)]
    named = jnp.logical_or(hot[0], hot[1]).astype(BF)
    earlier = (lanes((count, count)) < rows_of((count, count))).astype(BF)
    place = mm(earlier, named)
    dispatch = []
    column = lanes((count, groups * MOST))
    for choice in range(2):
        route = routes[:, choice : choice + 1]
        slot = jnp.sum(jnp.where(hot[choice], place, 0.0), axis=-1, keepdims=True)
        target = jnp.where(route < groups, route * MOST + slot.astype(jnp.int32), -1)
        dispatch.append((column == target).astype(BF))
    return gates, hot, dispatch


def route_kernel(where, att, out_weight, tok, small, small_t, resid, routes, cot, hidden_ref, low_ref, *rest, groups, gain_at):
    sends = rest[:groups]
    rows_x, rows_g = rest[groups], rest[groups + 1]
    hidden = tok[...].astype(F32) + mm(att[...], out_weight[...])
    hidden_ref[...] = hidden
    low = ((hidden * rms_scale(hidden)) * small_t[gain_at : gain_at + 1, :]).astype(BF)
    low_ref[...] = low
    logits = mm(low, small[...])
    gates, _, dispatch = routing(routes[...], resid[...].astype(F32), logits, groups)
    grad = cot[...].astype(F32)
    rows_x[...] = mm_tn(dispatch[0] + dispatch[1], low).astype(BF)
    rows_g[...] = (
        mm_tn(dispatch[0], (gates[0] * grad).astype(BF))
        + mm_tn(dispatch[1], (gates[1] * grad).astype(BF))
    ).astype(BF)
    for slot in range(groups):
        source = pl.ds(pl.multiple_of(where[slot] * MOST, MOST), MOST)
        sends[slot][:MOST, :] = rows_x[source, :]
        sends[slot][MOST:, :] = rows_g[source, :]


def expert_kernel(*refs, groups, hidden_units):
    own, other = refs[:groups], refs[groups : 2 * groups]
    gate_up, down = refs[2 * groups], refs[2 * groups + 1]
    own_out = refs[2 * groups + 2 : 3 * groups + 2]
    other_out = refs[3 * groups + 2 : 4 * groups + 2]
    grad_gate_up, grad_down = refs[4 * groups + 2], refs[4 * groups + 3]
    rows, grads, out_rows, back_rows = refs[4 * groups + 4 :]
    for index, ref in enumerate(own + other):
        target = slice(index * MOST, (index + 1) * MOST)
        rows[target, :] = ref[:MOST, :]
        grads[target, :] = ref[MOST:, :]
    x, g = rows[...], grads[...]
    chunk = 256
    for at in range(0, hidden_units, chunk):
        gate_w = gate_up[:, at : at + chunk]
        up_w = gate_up[:, hidden_units + at : hidden_units + at + chunk]
        down_w = down[at : at + chunk, :]
        gate, up = mm(x, gate_w), mm(x, up_w)
        sig = 1.0 / (1.0 + jnp.exp(-gate))
        silu = gate * sig
        act = (silu * up).astype(BF)
        grad_act = mm_nt(g, down_w)
        grad_gate = (grad_act * up * sig * (1.0 + gate * (1.0 - sig))).astype(BF)
        grad_up = (grad_act * silu).astype(BF)
        part_out = mm(act, down_w)
        part_back = mm_nt(grad_gate, gate_w) + mm_nt(grad_up, up_w)
        if at == 0:
            out_rows[...] = part_out
            back_rows[...] = part_back
        else:
            out_rows[...] += part_out
            back_rows[...] += part_back
        grad_gate_up[:, at : at + chunk] = mm_tn(x, grad_gate).astype(BF)
        grad_gate_up[:, hidden_units + at : hidden_units + at + chunk] = mm_tn(x, grad_up).astype(BF)
        grad_down[at : at + chunk, :] = mm_tn(act, g).astype(BF)
    for index, ref in enumerate(own_out + other_out):
        source = slice(index * MOST, (index + 1) * MOST)
        ref[:MOST, :] = out_rows[source, :].astype(ref.dtype)
        ref[MOST:, :] = back_rows[source, :].astype(ref.dtype)


def combine_kernel(where, *refs, groups, columns, shard_rows):
    backs = refs[:groups]
    (hidden_ref, low_ref, cot, routes, resid, small, small_t, out_weight, att,
     out_ref, grad_hidden_ref, grad_att_ref, grad_left, grad_right, grad_small, grad_resid,
     rows_y, rows_d) = refs[groups:]
    kinds, mix_at, value_at, gain_one_at, gain_two_at, square_at = columns
    for slot in range(groups):
        target = pl.ds(pl.multiple_of(where[slot] * MOST, MOST), MOST)
        rows_y[target, :] = backs[slot][:MOST, :]
        rows_d[target, :] = backs[slot][MOST:, :]
    hidden, low = hidden_ref[...], low_ref[...]
    count = low.shape[0]
    normed_input = low.astype(F32)
    grad_low_type = cot[...]
    grad = grad_low_type.astype(F32)
    logits = mm(low, small[...])
    grad_small_dot = mm(grad_low_type, small[...])
    route = routes[...]
    gates, hot, dispatch = routing(route, resid[...].astype(F32), logits, groups)
    returned = [mm(dispatch[c], rows_y[...]) for c in range(2)]
    grad_back = mm(dispatch[0] + dispatch[1], rows_d[...])
    grad_dot = jnp.sum(grad * normed_input, axis=-1, keepdims=True)
    is_copy = [(route[:, c : c + 1] == groups + 1).astype(F32) for c in range(2)]
    grad_gates = [
        jnp.sum(grad * returned[c], axis=-1, keepdims=True) + is_copy[c] * grad_dot
        for c in range(2)
    ]
    direct = gates[0] * is_copy[0] + gates[1] * is_copy[1]
    mixture = gates[0] * returned[0] + gates[1] * returned[1]
    lane = lanes((count, SMALL))
    grad_logits = jnp.zeros((count, SMALL), F32)
    value_weights = jnp.zeros((count, SMALL), F32)
    for const in range(NCONST):
        first = logits[:, mix_at + 2 * const : mix_at + 2 * const + 1]
        second = logits[:, mix_at + 2 * const + 1 : mix_at + 2 * const + 2]
        top = jnp.maximum(first, second)
        first, second = jnp.exp(first - top), jnp.exp(second - top)
        mix = [first / (first + second), second / (first + second)]
        value_dot = grad_small_dot[:, value_at + const : value_at + const + 1]
        named = [(route[:, c : c + 1] == groups + 2 + const).astype(F32) for c in range(2)]
        for c in range(2):
            grad_gates[c] += named[c] * (mix[0] * grad_dot + mix[1] * value_dot)
        weight = gates[0] * named[0] + gates[1] * named[1]
        direct += weight * mix[0]
        of_value = weight * mix[1]
        mixture += of_value * small_t[value_at + const : value_at + const + 1, :]
        value_weights = jnp.where(lane == value_at + const, of_value, value_weights)
        grad_mix = [weight * grad_dot, weight * value_dot]
        common = mix[0] * grad_mix[0] + mix[1] * grad_mix[1]
        for c in range(2):
            grad_logits = jnp.where(
                lane == mix_at + 2 * const + c, mix[c] * (grad_mix[c] - common), grad_logits
            )
    outputs = hidden + mixture + direct * normed_input
    out_ref[...] = outputs.astype(BF)
    common = gates[0] * grad_gates[0] + gates[1] * grad_gates[1]
    for c in range(2):
        grad_logits = jnp.where(hot[c], gates[c] * (grad_gates[c] - common), grad_logits)
    grad_resid[...] = grad_logits[:, :kinds].astype(BF)
    high, rest = split_low(grad_logits)
    weights = small[...]
    grad_low = grad_back + direct * grad + mm_nt(high, weights) + mm_nt(rest, weights)
    scale = rms_scale(hidden)
    normed = hidden * scale
    of_gain = split_low(grad_low * normed)
    ones = (lane == gain_two_at).astype(BF)
    value_high, value_rest = split_low(value_weights)
    summed = (
        mm_tn(low, high)
        + mm_tn(low, rest)
        + mm_tn(grad_low_type, value_high)
        + mm_tn(grad_low_type, value_rest)
        + mm_tn(of_gain[0], ones)
        + mm_tn(of_gain[1], ones)
    )
    column, row = lanes(summed.shape), rows_of(summed.shape)
    mine = row // shard_rows == where[groups]
    for index, total in enumerate((jnp.sum(hidden * hidden), jnp.sum(outputs * outputs))):
        for part, value in enumerate(split_low(jnp.full((1, 1), total, F32))):
            spot = jnp.logical_and(mine, column == square_at + 2 * index + part)
            summed = jnp.where(spot, value.astype(F32), summed)
    grad_small[...] = summed.astype(BF)
    grad_normed = grad_low * small_t[gain_two_at : gain_two_at + 1, :]
    grad_hidden = grad + scale * (
        grad_normed - normed * jnp.mean(grad_normed * normed, axis=-1, keepdims=True)
    )
    grad_hidden_ref[...] = grad_hidden
    branch = grad_hidden.astype(BF)
    grad_att_ref[...] = mm_nt(branch, out_weight[...]).astype(BF)
    grad_out = mm_tn(att[...], branch).astype(BF)
    middle = grad_out.shape[1] // 2
    grad_left[...] = grad_out[:, :middle]
    grad_right[...] = grad_out[:, middle:]


def project_back_kernel(where, tok, normed, dq, dk, dv, weight, left, right, rows_back, own_back, total, gain_total, *, slots, gain_at):
    step = pl.program_id(0)
    rank = where[step]
    own = where[slots]
    width = tok.shape[1]

    @pl.when(step == 0)
    def _():
        total[...] = jnp.zeros_like(total)
        gain_total[...] = jnp.zeros_like(gain_total)

    @pl.when(rank > own)
    def _():
        rows_back[...] = jnp.zeros_like(rows_back)

    @pl.when(rank <= own)
    def _():
        low = normed[...]
        x = tok[...].astype(F32)
        unit = x * rms_scale(x)
        grad_k, grad_v = dk[...], dv[...]
        total[:, width : 2 * width] += mm_tn(low, grad_k)
        total[:, 2 * width :] += mm_tn(low, grad_v)
        back = mm_nt(grad_k, weight[:, width : 2 * width]) + mm_nt(grad_v, weight[:, 2 * width :])
        rows_back[...] = back.astype(BF)
        gain_total[...] += jnp.sum((back * unit).reshape(-1, 8, width), axis=0)

        @pl.when(rank == own)
        def _():
            grad_q = dq[...]
            total[:, :width] += mm_tn(low, grad_q)
            mine = mm_nt(grad_q, weight[:, :width])
            own_back[...] = mine
            gain_total[...] += jnp.sum((mine * unit).reshape(-1, 8, width), axis=0)

    @pl.when(step == slots - 1)
    def _():
        half = left.shape[1]
        ones = (lanes((8, SMALL)) == gain_at).astype(BF)
        high, rest = split_low(gain_total[...])
        extra = mm_tn(high, ones) + mm_tn(rest, ones)
        left[...] = total[:, :half].astype(BF)
        right[:, : 3 * width - half] = total[:, half:].astype(BF)
        right[:, 3 * width - half :] = extra.astype(BF)


def finish_kernel(tok, small_t, grad_hidden, own_back, rows_back, out, *, gain_at):
    x = tok[...].astype(F32)
    scale = rms_scale(x)
    normed = x * scale
    grad = (own_back[...] + rows_back[...]) * small_t[gain_at : gain_at + 1, :]
    out[...] = (
        grad_hidden[...]
        + scale * (grad - normed * jnp.mean(grad * normed, axis=-1, keepdims=True))
    ).astype(BF)


def on_device(
    tokens,
    gain_one,
    qkv_weight,
    out_weight,
    gain_two,
    router_weight,
    const_gate,
    const_value,
    expert_gate_up,
    expert_down,
    gate_residual,
    routes,
    cotangent,
):
    parts = lax.axis_size("fsdp")
    groups = lax.axis_size("expert")
    me_fsdp = lax.axis_index("fsdp")
    me_expert = lax.axis_index("expert")
    minor = me_fsdp % 2
    major_count = parts // 2
    tok = tokens[0]
    count, width = tok.shape
    length = groups * count
    pairs = width // PAIR
    kinds = router_weight.shape[1]
    mix_at, value_at = kinds, kinds + 2 * NCONST
    gain_one_at = value_at + NCONST
    gain_two_at = gain_one_at + 1
    square_at = gain_two_at + 1
    shard_rows = width // parts

    tok_all, ranks = sequence_gather(tok)
    where = jnp.stack([jnp.asarray(r, jnp.int32) for r in ranks] + [me_expert.astype(jnp.int32)])

    unit = FF // parts
    halves = expert_gate_up[0].reshape(shard_rows, 2, major_count, 2, unit)
    away = lax.dynamic_index_in_dim(halves, 1 - minor, 3, False).reshape(shard_rows, FF)
    kept = lax.dynamic_index_in_dim(halves, minor, 3, False).reshape(shard_rows, FF)
    arrived = swap(away, "fsdp", 1)
    gate_up_rows = jnp.concatenate(
        [jnp.where(minor == 0, kept, arrived), jnp.where(minor == 0, arrived, kept)], axis=0
    )

    small_shard = jnp.concatenate(
        [
            router_weight,
            const_gate,
            const_value,
            gain_one[:, None],
            gain_two[:, None],
            jnp.zeros((shard_rows, SMALL - square_at), BF),
        ],
        axis=1,
    )
    (qkv_full, out_full, small), stage = shared_gather(qkv_weight, out_weight, small_shard)
    small_t = small.astype(F32).T[:32]

    down_rows = expert_down[0]
    if stage is not None:
        gate_up_rows = after(gate_up_rows, *stage)
        down_rows = after(down_rows, *stage)
    gate_up_half = major_gather(gate_up_rows)
    down_half = major_gather(down_rows)

    frequency = 10000.0 ** (-jnp.arange(HEAD // 2, dtype=F32) / (HEAD // 2))
    angles = jnp.arange(length, dtype=F32)[:, None] * frequency[None, :]
    cosine, sine = jnp.cos(angles), jnp.sin(angles)
    cosine = jnp.concatenate([cosine, cosine, cosine, cosine], axis=1)
    sine = jnp.concatenate([-sine, sine, -sine, sine], axis=1)

    at_rank = lambda j, w: (w[j], 0)
    fixed = lambda j, w: (0, 0)
    q, k_all, v_all, normed_all = call(
        functools.partial(project_kernel, slots=groups, gain_at=gain_one_at),
        [
            shaped((count, width), BF),
            shaped((length, width), BF),
            shaped((length, width), BF),
            shaped((length, width), BF),
        ],
        (where, tok_all, qkv_full, small_t, cosine, sine),
        grid=(groups,),
        in_specs=[
            pl.BlockSpec((count, width), lambda j, w: (j, 0)),
            pl.BlockSpec((width, 3 * width), fixed),
            pl.BlockSpec((32, width), fixed),
            pl.BlockSpec((count, PAIR), at_rank),
            pl.BlockSpec((count, PAIR), at_rank),
        ],
        out_specs=[
            pl.BlockSpec((count, width), fixed),
            pl.BlockSpec((count, width), at_rank),
            pl.BlockSpec((count, width), at_rank),
            pl.BlockSpec((count, width), at_rank),
        ],
        name="project",
    )
    head_rows = pl.BlockSpec((count, PAIR), lambda h, w: (0, h))
    head_keys = pl.BlockSpec((length, PAIR), lambda h, w: (0, h))
    head_log = pl.BlockSpec((1, 8, 2 * count), lambda h, w: (h, 0, 0))
    attended, log_total = call(
        functools.partial(attend_kernel, slots=groups),
        [shaped((count, width), BF), shaped((pairs, 8, 2 * count), F32)],
        (where, q, k_all, v_all),
        grid=(pairs,),
        in_specs=[head_rows, head_keys, head_keys],
        out_specs=[head_rows, head_log],
        name="attend",
    )

    residual = gate_residual[0]
    route = routes[0]
    cot = cotangent[0]
    slots = jnp.stack([(me_expert ^ j).astype(jnp.int32) for j in range(groups)] + [me_fsdp.astype(jnp.int32)])
    packed = shaped((2 * MOST, width), BF)
    hidden, low_two, *sends = call(
        functools.partial(route_kernel, groups=groups, gain_at=gain_two_at),
        [shaped((count, width), F32), shaped((count, width), BF)] + [packed] * groups,
        (slots, attended, out_full, tok, small, small_t, residual, route, cot),
        scratch=[pltpu.VMEM((groups * MOST, width), BF)] * 2,
        name="route",
    )
    received = [sends[0]] + [swap(sends[j], "expert", j) for j in range(1, groups)]
    others = [swap(v, "fsdp", 1) for v in received]
    units = FF // 2
    rows_total = 2 * groups * MOST
    results = call(
        functools.partial(expert_kernel, groups=groups, hidden_units=units),
        [shaped((2 * MOST, width), F32)] * groups
        + [packed] * groups
        + [shaped((width, 2 * units), BF), shaped((units, width), BF)],
        tuple(received) + tuple(others) + (gate_up_half, down_half),
        scratch=[pltpu.VMEM((rows_total, width), BF)] * 2
        + [pltpu.VMEM((rows_total, width), F32)] * 2,
        scalars=0,
        name="expert",
    )
    own_part, other_part = results[:groups], results[groups : 2 * groups]
    grad_gate_up, grad_down = results[2 * groups :]
    joined = [
        (a + swap(b, "fsdp", 1).astype(F32)).astype(BF) for a, b in zip(own_part, other_part)
    ]
    backs = [joined[0]] + [swap(joined[j], "expert", j) for j in range(1, groups)]

    shard_down = major_scatter_sum(grad_down)
    part = major_scatter_sum(grad_gate_up).reshape(2, shard_rows, FF)
    away = lax.dynamic_index_in_dim(part, 1 - minor, 0, False).astype(BF)
    kept = lax.dynamic_index_in_dim(part, minor, 0, False)
    arrived = swap(away, "fsdp", 1).astype(F32)
    first = jnp.where(minor == 0, kept, arrived).reshape(shard_rows, 2, major_count, 1, unit)
    second = jnp.where(minor == 0, arrived, kept).reshape(shard_rows, 2, major_count, 1, unit)
    shard_gate_up = jnp.concatenate([first, second], axis=3).reshape(shard_rows, 2 * FF)

    columns = (kinds, mix_at, value_at, gain_one_at, gain_two_at, square_at)
    outputs, grad_hidden, grad_att, out_left, out_right, grad_small, grad_residual = call(
        functools.partial(combine_kernel, groups=groups, columns=columns, shard_rows=shard_rows),
        [
            shaped((count, width), BF),
            shaped((count, width), F32),
            shaped((count, width), BF),
            shaped((width, width // 2), BF),
            shaped((width, width // 2), BF),
            shaped((width, SMALL), BF),
            shaped((count, kinds), BF),
        ],
        (slots,) + tuple(backs)
        + (hidden, low_two, cot, route, residual, small, small_t, out_full, attended),
        scratch=[pltpu.VMEM((groups * MOST, width), BF)] * 2,
        name="combine",
    )
    out_sum = shared_scatter_sum(
        jnp.concatenate([out_left, grad_small], axis=1),
        jnp.concatenate([out_right, jnp.zeros_like(grad_small)], axis=1),
    )
    own_rows = pl.BlockSpec((count, PAIR), lambda h, w: (w[groups], 0))
    all_rows = pl.BlockSpec((length, PAIR), lambda h, w: (0, 0))
    dq, dk, dv = call(
        functools.partial(attend_back_kernel, slots=groups),
        [shaped((count, width), BF), shaped((length, width), BF), shaped((length, width), BF)],
        (where, q, k_all, v_all, grad_att, log_total, cosine, sine, cosine, sine),
        grid=(pairs,),
        in_specs=[head_rows, head_keys, head_keys, head_rows, head_log, all_rows, all_rows, own_rows, own_rows],
        out_specs=[head_rows, head_keys, head_keys],
        name="attend_back",
    )
    half = 3 * width // 2 + SMALL // 2
    half = (half + 127) // 128 * 128
    left, right, rows_back, own_back = call(
        functools.partial(project_back_kernel, slots=groups, gain_at=gain_one_at),
        [
            shaped((width, half), BF),
            shaped((width, 3 * width + SMALL - half), BF),
            shaped((length, width), BF),
            shaped((count, width), F32),
        ],
        (where, tok_all, normed_all, dq, dk, dv, qkv_full),
        grid=(groups,),
        in_specs=[
            pl.BlockSpec((count, width), lambda j, w: (j, 0)),
            pl.BlockSpec((count, width), at_rank),
            pl.BlockSpec((count, width), fixed),
            pl.BlockSpec((count, width), at_rank),
            pl.BlockSpec((count, width), at_rank),
            pl.BlockSpec((width, 3 * width), fixed),
        ],
        out_specs=[
            pl.BlockSpec((width, half), fixed),
            pl.BlockSpec((width, 3 * width + SMALL - half), fixed),
            pl.BlockSpec((count, width), at_rank),
            pl.BlockSpec((count, width), fixed),
        ],
        scratch=[pltpu.VMEM((width, 3 * width), F32), pltpu.VMEM((8, width), F32)],
        name="project_back",
    )
    if right.shape[1] < half:
        right = jnp.concatenate([right, jnp.zeros((width, half - right.shape[1]), BF)], axis=1)
    qkv_sum = shared_scatter_sum(left, right)
    rows_sum = sequence_scatter_sum(rows_back, count)
    grad_tokens = call(
        functools.partial(finish_kernel, gain_at=gain_one_at),
        shaped((count, width), BF),
        (tok, small_t, grad_hidden, own_back, rows_sum),
        scalars=0,
        name="finish",
    )

    small_sum = out_sum[:, width // 2 : width // 2 + SMALL]
    shard_out = jnp.concatenate(
        [out_sum[:, : width // 2], out_sum[:, width // 2 + SMALL : width + SMALL]], axis=1
    )
    squares = small_sum[0, square_at : square_at + 4]
    stream = jnp.sqrt(
        jnp.stack([squares[0] + squares[1], squares[2] + squares[3]]) / (length * width)
    )
    return (
        outputs[None],
        grad_tokens[None],
        qkv_sum[:, 3 * width + gain_one_at],
        qkv_sum[:, : 3 * width],
        shard_out,
        small_sum[:, gain_two_at],
        small_sum[:, :kinds],
        small_sum[:, mix_at : mix_at + 2 * NCONST],
        small_sum[:, value_at : value_at + NCONST],
        shard_gate_up[None],
        shard_down[None],
        grad_residual[None],
        stream[None],
    )


def solution(mesh):
    return jax.shard_map(
        on_device,
        mesh=mesh,
        in_specs=(
            P("fsdp", "expert", None),
            P("fsdp"),
            P("fsdp", None),
            P("fsdp", None),
            P("fsdp"),
            P("fsdp", None),
            P("fsdp", None),
            P("fsdp", None),
            P("expert", "fsdp", None),
            P("expert", "fsdp", None),
            P("fsdp", "expert", None),
            P("fsdp", "expert", None),
            P("fsdp", "expert", None),
        ),
        out_specs=(
            P("fsdp", "expert", None),
            P("fsdp", "expert", None),
            P("fsdp"),
            P("fsdp", None),
            P("fsdp", None),
            P("fsdp"),
            P("fsdp", None),
            P("fsdp", None),
            P("fsdp", None),
            P("expert", "fsdp", None),
            P("expert", "fsdp", None),
            P("fsdp", "expert", None),
            P("fsdp", None),
        ),
        check_vma=False,
    )
```

time: 1040 us -> 456 us (0.44)
  waiting for transfers between devices: 619 us -> 179 us
  matrix products: 136 us -> 0 us
  blocking collectives: 125 us -> 0 us
  Pallas kernels: 0 us -> 93.8 us
  starting transfers between devices: 16.2 us -> 97.3 us
  local copies, waits for them, and re-layouts: 71.9 us -> 46.6 us
  between operations: 18.1 us -> 4.19 us
  other arithmetic: 42.6 us -> 30.7 us
    reduce_scatter x4 -> x0, waiting for transfers between devices: 270 us -> none  [the longest x1 118 us: on_device(): lax.psum_scatter(grad_gate_up_w.astype(jnp.bfloat16), 'fsdp', scatter_dim...]
    unnamed x19 -> x0, waiting for transfers between devices: 184 us -> none
    ppermute x0 -> x58, waiting for transfers between devices: none -> 179 us  [the longest x16 90.8 us: along(): lax.ppermute(values, 'fsdp', [(2 * i + b, 2 * j + b) for i, j in pairs fo...]
    dot_general x33 -> x0, matrix products: 136 us -> none  [the longest x2 21.1 us: local_mixture(): jnp.einsum('...kc,...cd->...kd', onehot[..., expert_count + 2:], const_ou...]
    all_gather x8 -> x0, waiting for transfers between devices: 130 us -> none  [the longest x1 53.4 us: on_device(): lax.all_gather(expert_down[0], 'fsdp', axis=0, tiled=True)]
    ppermute x0 -> x58, starting transfers between devices: none -> 97.3 us  [the longest x42 52.5 us: swap(): return lax.ppermute(values, axis, [(i, i ^ bits) for i in range(size)])]
    pallas_call x0 -> x11, Pallas kernels: none -> 93.8 us  [call(): pl.pallas_call(kernel, out_shape=outs, grid_spec=pltpu.PrefetchScalarGrid...]
    all_gather x5 -> x0, blocking collectives: 74.2 us -> none  [the longest x1 26.1 us: on_device(): lax.all_gather(router_weight, 'fsdp', axis=0, tiled=True)]
  transfers between devices with their start and end apart: 20 -> 58, of which waited for: 12 -> 21; matrix products, arithmetic and copies ran while one was open for 20% -> 14% of each run, Pallas kernels for 0% -> 17%
where the time goes in v1:
time: 456 us; the launch traced here: 451 us
  waiting for transfers between devices  179 us (39%)
  starting transfers between devices  97.3 us (21%)
  Pallas kernels  93.8 us (21%)
  local copies, waits for them, and re-layouts  46.6 us (10%)
  other arithmetic  30.7 us (7%)
    pallas_call x11, Pallas kernels, call(): pl.pallas_call(kernel, out_shape=outs, grid_spec=pltpu.PrefetchScalarGrid...  93.8 us
    ppermute x16, waiting for transfers between devices, along(): lax.ppermute(values, 'fsdp', [(2 * i + b, 2 * j + b) for i, j in pairs fo...  90.8 us
    ppermute x42, waiting for transfers between devices, swap(): return lax.ppermute(values, axis, [(i, i ^ bits) for i in range(size)])  87.9 us
    ppermute x42, starting transfers between devices, swap(): return lax.ppermute(values, axis, [(i, i ^ bits) for i in range(size)])  52.5 us
    ppermute x16, starting transfers between devices, along(): lax.ppermute(values, 'fsdp', [(2 * i + b, 2 * j + b) for i, j in pairs fo...  44.7 us
    unnamed x93, local copies, waits for them, and re-layouts  14.8 us
  transfers between devices with their start and end apart: 58, of which 21 were waited for; matrix products, arithmetic and copies ran while one was open for 14% of the time, Pallas kernels for 17%

profile of v1, /device:TPU:0, one launch (start us, length us, event | category | flops | bytes accessed | tf_op | source)
XLA Modules:
  0.0 451.4 jit_solution(508625264032164056)
XLA Ops:
  13.9 8.6 %collective-permute-done.2 = bf16[96,1664]{1,0:T(8,128)(2,1)S(1)} collective-permute-done((bf16[96,1664]{1,0:T(8,128)(2,1)S(1)}, bf16[96,1664]{1,0:T(8,128)(2,1)S(1)}, u32[]{:S(2)}, u32[]{:S(2)}) %collective-permute-start.2) | collective-permute-done | bytes 319520 | tf_op jit(solution)/shard_map/ppermute | solution.py:90
  24.9 9.0 %collective-permute-done.3 = bf16[96,1664]{1,0:T(8,128)(2,1)S(1)} collective-permute-done((bf16[96,1664]{1,0:T(8,128)(2,1)S(1)}, bf16[96,1664]{1,0:T(8,128)(2,1)S(1)}, u32[]{:S(2)}, u32[]{:S(2)}) %collective-permute-start.3) | collective-permute-done | bytes 319520 | tf_op jit(solution)/shard_map/ppermute | solution.py:90
  46.2 4.9 %dynamic-slice_reduce_fusion.1 = (bf16[96,2,4,256]{3,2,1,0:T(4,128)(2,1)S(1)}, bf16[96,2,4,256]{3,2,1,0:T(4,128)(2,1)S(1)}) fusion(bf16[96,2,4,2,256]{4,3,2,1,0:T(2,128)(2,1)S(1)} %reshape_squeeze.3, s32[]{:T(128)S(6)} %select_n.180, s32[]{:T(128)S(6)} %select_n.181), kind=kLoop, calls=%fused_computation.25 | loop fusion | bytes 1572872 | tf_op jit(solution)/shard_map/jit(dynamic_index_in_dim)/dynamic_slice | solution.py:640
  54.6 8.4 %collective-permute-done.17 = bf16[96,2048]{1,0:T(8,128)(2,1)S(1)} collective-permute-done((bf16[96,2048]{1,0:T(8,128)(2,1)S(1)}, bf16[96,2048]{1,0:T(8,128)(2,1)S(1)}, u32[]{:S(2)}, u32[]{:S(2)}) %collective-permute-start.17) | collective-permute-done | bytes 393248 | tf_op jit(solution)/shard_map/ppermute | solution.py:90
  69.5 49.1 %collective-permute-done.23.far_ref = bf16[256,768]{1,0:T(8,128)(2,1)} collective-permute-done((bf16[256,768]{1,0:T(8,128)(2,1)}, bf16[256,768]{1,0:T(8,128)(2,1)}, u32[]{:S(2)}, u32[]{:S(2)}) %collective-permute-start.23) | collective-permute-done | bytes 393248 | tf_op jit(solution)/shard_map/ppermute | solution.py:94
  131.1 13.5 %collective-permute-start.21 = (bf16[192,2048]{1,0:T(8,128)(2,1)S(1)}, bf16[192,2048]{1,0:T(8,128)(2,1)}, u32[]{:S(2)}, u32[]{:S(2)}) collective-permute-start(bf16[192,2048]{1,0:T(8,128)(2,1)S(1)} %collective-permute-done.19.far_ref), channel_id=1, source_target_pairs={{4,6},{5,7},{2,0},{3,1},{12,14},{13,15},{10,8},{11,9},{20,22},{21,... | collective-permute-start | bytes 2359304 | tf_op jit(solution)/shard_map/ppermute | solution.py:94
  147.0 5.9 %place_shared.1 = (bf16[768,2304]{1,0:T(8,128)(2,1)}, bf16[768,768]{1,0:T(8,128)(2,1)}, bf16[768,128]{1,0:T(8,128)(2,1)}) custom-call(s32[9]{0:T(128)} %stack.101.where, bf16[768,1664]{1,0:T(8,128)(2,1)} %constant_dynamic-update-slice_fusion.own_ref, bf16[768,1664]{1,0:T(8,128)(2,1)} %collective-permute-done.9.other_ref), custom_call_target="tpu_custom_call" | custom-call | tf_op jit(solution)/shard_map/place_shared/pallas_call | solution.py:69
  154.6 8.0 %project.1 = (bf16[256,768]{1,0:T(8,128)(2,1)}, bf16[1024,768]{1,0:T(8,128)(2,1)}, bf16[1024,768]{1,0:T(8,128)(2,1)}, bf16[1024,768]{1,0:T(8,128)(2,1)}) custom-call(s32[5]{0:T(128)} %stack.92.where, bf16[1024,768]{1,0:T(8,128)(2,1)} %pad_maximum_fusion.tok, bf16[768,2304]{1,0:T(8,128)(2,1)} %get-tuple-element.54.weight, ...), custom_call_target="tpu_custom_call" | custom-call | tf_op jit(solution)/shard_map/project/pallas_call | solution.py:69
  162.6 12.3 %attend.1 = (bf16[256,768]{1,0:T(8,128)(2,1)}, f32[6,8,512]{2,1,0:T(8,128)}) custom-call(s32[5]{0:T(128)} %stack.92.where, bf16[256,768]{1,0:T(8,128)(2,1)} %get-tuple-element.56.q, bf16[1024,768]{1,0:T(8,128)(2,1)} %get-tuple-element.57.k, bf16[1024,768]{1,0:T(8,128)(2,1)} %get-tuple-element.58.v), custom_call_target="tpu_custom_call" | custom-call | tf_op jit(solution)/shard_map/attend/pallas_call | solution.py:69
  174.9 4.9 %route.1 = (f32[256,768]{1,0:T(8,128)}, bf16[256,768]{1,0:T(8,128)(2,1)}, bf16[160,768]{1,0:T(8,128)(2,1)}, bf16[160,768]{1,0:T(8,128)(2,1)}, bf16[160,768]{1,0:T(8,128)(2,1)}, /*index=5*/bf16[160,768]{1,0:T(8,128)(2,1)}) custom-call(s32[5]{0:T(128)} %stack.91.where, bf16[256,768]{1,0:T(8,128)(2,1)} %get-tuple-element.59.att.refs_12_, ...), custom_call_target="tpu_custom_call" | custom-call | tf_op jit(solution)/shard_map/route/pallas_call | solution.py:69
  184.8 4.8 %collective-permute-done.11.refs_2_ = bf16[160,768]{1,0:T(8,128)(2,1)S(1)} collective-permute-done((bf16[160,768]{1,0:T(8,128)(2,1)}, bf16[160,768]{1,0:T(8,128)(2,1)S(1)}, u32[]{:S(2)}, u32[]{:S(2)}) %collective-permute-start.11) | collective-permute-done | bytes 245792 | tf_op jit(solution)/shard_map/ppermute | solution.py:90
  199.9 4.7 %place_parts.2.refs_8_ = bf16[768,2048]{1,0:T(8,128)(2,1)} custom-call(s32[5]{0:T(128)} %stack.108.where, bf16[192,2048]{1,0:T(8,128)(2,1)} %copy-done.7, bf16[192,2048]{1,0:T(8,128)(2,1)} %copy-done.16, bf16[192,2048]{1,0:T(8,128)(2,1)} %copy-done.15, bf16[192,2048]{1,0:T(8,128)(2,1)} %collective-permute-done.20.middle_ref, ...), custom_call_target="tpu_custom_call" | custom-call | tf_op jit(solution)/shard_map/place_parts/pallas_call | solution.py:69
  206.9 16.0 %expert.1 = (f32[160,768]{1,0:T(8,128)}, f32[160,768]{1,0:T(8,128)}, f32[160,768]{1,0:T(8,128)}, f32[160,768]{1,0:T(8,128)}, bf16[160,768]{1,0:T(8,128)(2,1)}, /...) custom-call(bf16[160,768]{1,0:T(8,128)(2,1)} %get-tuple-element.61.r, ...), custom_call_target="tpu_custom_call" | custom-call | tf_op jit(solution)/shard_map/expert/pallas_call | solution.py:69
  224.9 8.3 %collective-permute-start.55 = (bf16[256,768]{1,0:T(8,128)(2,1)}, bf16[256,768]{1,0:T(8,128)(2,1)S(1)}, u32[]{:S(2)}, u32[]{:S(2)}) collective-permute-start(bf16[256,768]{1,0:T(8,128)(2,1)} %get-tuple-element.128), channel_id=1, source_target_pairs={{0,2},{1,3},{6,4},{7,5},{8,10},{9,11},{14,12},{15,13},{16,18},{17,... | collective-permute-start | bytes 1179656 | tf_op jit(solution)/shard_map/ppermute | solution.py:94
  249.0 5.2 %collective-permute-done.27 = bf16[160,768]{1,0:T(8,128)(2,1)S(1)} collective-permute-done((bf16[160,768]{1,0:T(8,128)(2,1)}, bf16[160,768]{1,0:T(8,128)(2,1)S(1)}, u32[]{:S(2)}, u32[]{:S(2)}) %collective-permute-start.27) | collective-permute-done | bytes 245792 | tf_op jit(solution)/shard_map/ppermute | solution.py:90
  260.5 4.8 %collective-permute-start.50 = (bf16[192,2048]{1,0:T(8,128)(2,1)}, bf16[192,2048]{1,0:T(8,128)(2,1)}, u32[]{:S(2)}, u32[]{:S(2)}) collective-permute-start(bf16[192,2048]{1,0:T(8,128)(2,1)} %get-tuple-element.124), channel_id=1, source_target_pairs={{0,2},{1,3},{6,4},{7,5},{8,10},{9,11},{14,12},{15,13},{16,18},{17,... | collective-permute-start | bytes 2359304 | tf_op jit(solution)/shard_map/ppermute | solution.py:94
  266.1 9.8 %combine.1 = (bf16[256,768]{1,0:T(8,128)(2,1)}, f32[256,768]{1,0:T(8,128)}, bf16[256,768]{1,0:T(8,128)(2,1)}, bf16[768,384]{1,0:T(8,128)(2,1)}, bf16[768,384]{1,...) custom-call(s32[5]{0:T(128)} %stack.91.where, bf16[160,768]{1,0:T(8,128)(2,1)} %add_convert_fusion.6.refs_0_, ...), custom_call_target="tpu_custom_call" | custom-call | tf_op jit(solution)/shard_map/combine/pallas_call | solution.py:69
  279.1 14.8 %attend_back.1 = (bf16[256,768]{1,0:T(8,128)(2,1)}, bf16[1024,768]{1,0:T(8,128)(2,1)}, bf16[1024,768]{1,0:T(8,128)(2,1)}) custom-call(s32[5]{0:T(128)} %stack.92.where, bf16[256,768]{1,0:T(8,128)(2,1)} %get-tuple-element.56.q, bf16[1024,768]{1,0:T(8,128)(2,1)} %get-tuple-element.57.k, bf16[1024,768]{1,0:T(8,128)(2,1)} %get-tuple-element.58.v, ...), custom_call_target="tpu_custom_call" | custom-call | tf_op jit(solution)/shard_map/attend_back/pallas_call | solution.py:69
  293.9 11.2 %project_back.1 = (bf16[768,1280]{1,0:T(8,128)(2,1)}, bf16[768,1152]{1,0:T(8,128)(2,1)}, bf16[1024,768]{1,0:T(8,128)(2,1)}, f32[256,768]{1,0:T(8,128)}) custom-call(s32[5]{0:T(128)} %stack.92.where, bf16[1024,768]{1,0:T(8,128)(2,1)} %pad_maximum_fusion.tok, bf16[1024,768]{1,0:T(8,128)(2,1)} %get-tuple-element.79.normed, ...), custom_call_target="tpu_custom_call" | custom-call | tf_op jit(solution)/shard_map/project_back/pallas_call | solution.py:69
  316.6 4.7 %collective-permute-start.49 = (bf16[192,2048]{1,0:T(8,128)(2,1)S(1)}, bf16[192,2048]{1,0:T(8,128)(2,1)S(1)}, u32[]{:S(2)}, u32[]{:S(2)}) collective-permute-start(bf16[192,2048]{1,0:T(8,128)(2,1)S(1)} %copy-done.18), channel_id=1, source_target_pairs={{0,2},{1,3},{2,0},{3,1},{4,6},{5,7},{6,4},{7,5},{8,10},{9,11},{10,... | collective-permute-start | bytes 2359304 | tf_op jit(solution)/shard_map/ppermute | solution.py:94
  327.1 12.3 %collective-permute-done.49 = bf16[192,2048]{1,0:T(8,128)(2,1)S(1)} collective-permute-done((bf16[192,2048]{1,0:T(8,128)(2,1)S(1)}, bf16[192,2048]{1,0:T(8,128)(2,1)S(1)}, u32[]{:S(2)}, u32[]{:S(2)}) %collective-permute-start.49) | collective-permute-done | bytes 786464 | tf_op jit(solution)/shard_map/ppermute | solution.py:94
  343.0 29.4 %collective-permute-done.51 = bf16[192,2048]{1,0:T(8,128)(2,1)S(1)} collective-permute-done((bf16[192,2048]{1,0:T(8,128)(2,1)S(1)}, bf16[192,2048]{1,0:T(8,128)(2,1)S(1)}, u32[]{:S(2)}, u32[]{:S(2)}) %collective-permute-start.51) | collective-permute-done | bytes 786464 | tf_op jit(solution)/shard_map/ppermute | solution.py:94
  401.3 10.3 %collective-permute-done.36 = bf16[4,96,1280]{2,1,0:T(8,128)(2,1)} collective-permute-done((bf16[4,96,1280]{2,1,0:T(8,128)(2,1)}, bf16[4,96,1280]{2,1,0:T(8,128)(2,1)}, u32[]{:S(2)}, u32[]{:S(2)}) %collective-permute-start.36) | collective-permute-done | bytes 983072 | tf_op jit(solution)/shard_map/ppermute | solution.py:90
  422.8 12.3 %collective-permute-done.38 = bf16[96,1280]{1,0:T(8,128)(2,1)S(1)} collective-permute-done((bf16[96,1280]{1,0:T(8,128)(2,1)S(1)}, bf16[96,1280]{1,0:T(8,128)(2,1)S(1)}, u32[]{:S(2)}, u32[]{:S(2)}) %collective-permute-start.38) | collective-permute-done | bytes 245792 | tf_op jit(solution)/shard_map/ppermute | solution.py:90
  (271 shorter events, 174.0 us)
Async XLA Ops:
  8.8 25.1 %collective-permute-start.3 = (bf16[96,1664]{1,0:T(8,128)(2,1)S(1)}, bf16[96,1664]{1,0:T(8,128)(2,1)S(1)}, u32[]{:S(2)}, u32[]{:S(2)}) collective-permute-start(bf16[96,1664]{1,0:T(8,128)(2,1)S(1)} %concatenate.58), channel_id=1, source_target_pairs={{0,4},{1,5},{2,6},{3,7},{4,0},{5,1},{6,2},{7,3},{8,12},{9,13},{10,... | collective-permute-start | bytes 958472 | tf_op jit(solution)/shard_map/ppermute | solution.py:90
  11.4 24.7 %collective-permute-start.4 = (bf16[96,1664]{1,0:T(8,128)(2,1)S(1)}, bf16[96,1664]{1,0:T(8,128)(2,1)S(1)}, u32[]{:S(2)}, u32[]{:S(2)}) collective-permute-start(bf16[96,1664]{1,0:T(8,128)(2,1)S(1)} %concatenate.58), channel_id=1, source_target_pairs={{0,6},{1,7},{2,4},{3,5},{4,2},{5,3},{6,0},{7,1},{8,14},{9,15},{10,... | collective-permute-start | bytes 958472 | tf_op jit(solution)/shard_map/ppermute | solution.py:90
  11.4 26.0 %collective-permute-start.5 = (bf16[96,1664]{1,0:T(8,128)(2,1)S(1)}, bf16[96,1664]{1,0:T(8,128)(2,1)S(1)}, u32[]{:S(2)}, u32[]{:S(2)}) collective-permute-start(bf16[96,1664]{1,0:T(8,128)(2,1)S(1)} %concatenate.58), channel_id=1, source_target_pairs={{0,1},{1,0},{2,3},{3,2},{4,5},{5,4},{6,7},{7,6},{8,9},{9,8},{10,11... | collective-permute-start | bytes 958472 | tf_op jit(solution)/shard_map/ppermute | solution.py:90
  45.6 85.5 %collective-permute-start.9 = (bf16[768,1664]{1,0:T(8,128)(2,1)}, bf16[768,1664]{1,0:T(8,128)(2,1)}, u32[]{:S(2)}, u32[]{:S(2)}) collective-permute-start(bf16[768,1664]{1,0:T(8,128)(2,1)} %constant_dynamic-update-slice_fusion.own_ref), channel_id=1, source_target_pairs={{0,8},{8,0},{16,24},{24,16},{1,9},{9,1},{17,25},{25,17},{2,10},{10... | collective-permute-start | bytes 7667720 | tf_op jit(solution)/shard_map/ppermute | solution.py:90
  63.2 59.1 %collective-permute-start.19 = (bf16[192,2048]{1,0:T(8,128)(2,1)S(1)}, bf16[192,2048]{1,0:T(8,128)(2,1)S(1)}, u32[]{:S(2)}, u32[]{:S(2)}) collective-permute-start(bf16[192,2048]{1,0:T(8,128)(2,1)S(1)} %pad_maximum_fusion.3.own), channel_id=1, source_target_pairs={{0,4},{1,5},{4,0},{5,1},{2,6},{3,7},{6,2},{7,3},{8,12},{9,13},{12,... | collective-permute-start | bytes 2359304 | tf_op jit(solution)/shard_map/ppermute | solution.py:94
  67.4 56.2 %collective-permute-start.1 = (bf16[512,768]{1,0:T(8,128)(2,1)S(1)}, bf16[512,768]{1,0:T(8,128)(2,1)S(1)}, u32[]{:S(2)}, u32[]{:S(2)}) collective-permute-start(bf16[512,768]{1,0:T(8,128)(2,1)S(1)} %pad_maximum_fusion.2), channel_id=1, source_target_pairs={{0,8},{8,0},{16,24},{24,16},{1,9},{9,1},{17,25},{25,17},{2,10},{10... | collective-permute-start | bytes 2359304 | tf_op jit(solution)/shard_map/ppermute | solution.py:90
  67.5 51.1 %collective-permute-start.23 = (bf16[256,768]{1,0:T(8,128)(2,1)}, bf16[256,768]{1,0:T(8,128)(2,1)}, u32[]{:S(2)}, u32[]{:S(2)}) collective-permute-start(bf16[256,768]{1,0:T(8,128)(2,1)} %bitcast.25.own), channel_id=1, source_target_pairs={{0,4},{1,5},{4,0},{5,1},{2,6},{3,7},{6,2},{7,3},{8,12},{9,13},{12,... | collective-permute-start | bytes 1179656 | tf_op jit(solution)/shard_map/ppermute | solution.py:94
  68.6 50.1 %collective-permute-start.22 = (bf16[256,768]{1,0:T(8,128)(2,1)}, bf16[256,768]{1,0:T(8,128)(2,1)S(1)}, u32[]{:S(2)}, u32[]{:S(2)}) collective-permute-start(bf16[256,768]{1,0:T(8,128)(2,1)} %bitcast.25.own), channel_id=1, source_target_pairs={{0,2},{1,3},{2,0},{3,1},{4,6},{5,7},{6,4},{7,5},{8,10},{9,11},{10,... | collective-permute-start | bytes 1179656 | tf_op jit(solution)/shard_map/ppermute | solution.py:94
  118.6 64.0 %collective-permute-start.18 = (bf16[192,2048]{1,0:T(8,128)(2,1)S(1)}, bf16[192,2048]{1,0:T(8,128)(2,1)S(1)}, u32[]{:S(2)}, u32[]{:S(2)}) collective-permute-start(bf16[192,2048]{1,0:T(8,128)(2,1)S(1)} %pad_maximum_fusion.3.own), channel_id=1, source_target_pairs={{0,2},{1,3},{2,0},{3,1},{4,6},{5,7},{6,4},{7,5},{8,10},{9,11},{10,... | collective-permute-start | bytes 2359304 | tf_op jit(solution)/shard_map/ppermute | solution.py:94
  118.7 64.1 %collective-permute-start.20 = (bf16[192,2048]{1,0:T(8,128)(2,1)S(1)}, bf16[192,2048]{1,0:T(8,128)(2,1)}, u32[]{:S(2)}, u32[]{:S(2)}) collective-permute-start(bf16[192,2048]{1,0:T(8,128)(2,1)S(1)} %pad_maximum_fusion.3.own), channel_id=1, source_target_pairs={{2,4},{3,5},{4,2},{5,3},{10,12},{11,13},{12,10},{13,11},{18,20},{1... | collective-permute-start | bytes 2359304 | tf_op jit(solution)/shard_map/ppermute | solution.py:94
  122.2 57.6 %collective-permute-start.24 = (bf16[256,768]{1,0:T(8,128)(2,1)}, bf16[256,768]{1,0:T(8,128)(2,1)}, u32[]{:S(2)}, u32[]{:S(2)}) collective-permute-start(bf16[256,768]{1,0:T(8,128)(2,1)} %bitcast.25.own), channel_id=1, source_target_pairs={{2,4},{3,5},{4,2},{5,3},{10,12},{11,13},{12,10},{13,11},{18,20},{1... | collective-permute-start | bytes 1179656 | tf_op jit(solution)/shard_map/ppermute | solution.py:94
  124.6 55.3 %collective-permute-start.25 = (bf16[256,768]{1,0:T(8,128)(2,1)}, bf16[256,768]{1,0:T(8,128)(2,1)}, u32[]{:S(2)}, u32[]{:S(2)}) collective-permute-start(bf16[256,768]{1,0:T(8,128)(2,1)} %collective-permute-done.23.far_ref), channel_id=1, source_target_pairs={{4,6},{5,7},{2,0},{3,1},{12,14},{13,15},{10,8},{11,9},{20,22},{21,... | collective-permute-start | bytes 1179656 | tf_op jit(solution)/shard_map/ppermute | solution.py:94
  131.1 68.8 %collective-permute-start.21 = (bf16[192,2048]{1,0:T(8,128)(2,1)S(1)}, bf16[192,2048]{1,0:T(8,128)(2,1)}, u32[]{:S(2)}, u32[]{:S(2)}) collective-permute-start(bf16[192,2048]{1,0:T(8,128)(2,1)S(1)} %collective-permute-done.19.far_ref), channel_id=1, source_target_pairs={{4,6},{5,7},{2,0},{3,1},{12,14},{13,15},{10,8},{11,9},{20,22},{21,... | collective-permute-start | bytes 2359304 | tf_op jit(solution)/shard_map/ppermute | solution.py:94
  224.9 33.3 %collective-permute-start.55 = (bf16[256,768]{1,0:T(8,128)(2,1)}, bf16[256,768]{1,0:T(8,128)(2,1)S(1)}, u32[]{:S(2)}, u32[]{:S(2)}) collective-permute-start(bf16[256,768]{1,0:T(8,128)(2,1)} %get-tuple-element.128), channel_id=1, source_target_pairs={{0,2},{1,3},{6,4},{7,5},{8,10},{9,11},{14,12},{15,13},{16,18},{17,... | collective-permute-start | bytes 1179656 | tf_op jit(solution)/shard_map/ppermute | solution.py:94
  233.2 83.4 %collective-permute-start.57 = (bf16[256,768]{1,0:T(8,128)(2,1)}, bf16[256,768]{1,0:T(8,128)(2,1)}, u32[]{:S(2)}, u32[]{:S(2)}) collective-permute-start(bf16[256,768]{1,0:T(8,128)(2,1)} %get-tuple-element.128), channel_id=1, source_target_pairs={{2,4},{3,5},{4,2},{5,3},{10,12},{11,13},{12,10},{13,11},{18,20},{1... | collective-permute-start | bytes 1179656 | tf_op jit(solution)/shard_map/ppermute | solution.py:94
  258.2 57.4 %collective-permute-start.54 = (bf16[256,768]{1,0:T(8,128)(2,1)}, bf16[256,768]{1,0:T(8,128)(2,1)}, u32[]{:S(2)}, u32[]{:S(2)}) collective-permute-start(bf16[256,768]{1,0:T(8,128)(2,1)} %get-tuple-element.127), channel_id=1, source_target_pairs={{0,2},{1,3},{2,0},{3,1},{4,6},{5,7},{6,4},{7,5},{8,10},{9,11},{10,... | collective-permute-start | bytes 1179656 | tf_op jit(solution)/shard_map/ppermute | solution.py:94
  260.5 51.9 %collective-permute-start.50 = (bf16[192,2048]{1,0:T(8,128)(2,1)}, bf16[192,2048]{1,0:T(8,128)(2,1)}, u32[]{:S(2)}, u32[]{:S(2)}) collective-permute-start(bf16[192,2048]{1,0:T(8,128)(2,1)} %get-tuple-element.124), channel_id=1, source_target_pairs={{0,2},{1,3},{6,4},{7,5},{8,10},{9,11},{14,12},{15,13},{16,18},{17,... | collective-permute-start | bytes 2359304 | tf_op jit(solution)/shard_map/ppermute | solution.py:94
  265.3 56.0 %collective-permute-start.56 = (bf16[256,768]{1,0:T(8,128)(2,1)}, bf16[256,768]{1,0:T(8,128)(2,1)}, u32[]{:S(2)}, u32[]{:S(2)}) collective-permute-start(bf16[256,768]{1,0:T(8,128)(2,1)} %dynamic-slice_add_fusion.1), channel_id=1, source_target_pairs={{0,4},{1,5},{4,0},{5,1},{2,6},{3,7},{6,2},{7,3},{8,12},{9,13},{12,... | collective-permute-start | bytes 1179656 | tf_op jit(solution)/shard_map/ppermute | solution.py:94
  279.1 44.7 %collective-permute-start.42 = (bf16[768,512]{1,0:T(8,128)(2,1)}, bf16[768,512]{1,0:T(8,128)(2,1)}, u32[]{:S(2)}, u32[]{:S(2)}) collective-permute-start(bf16[768,512]{1,0:T(8,128)(2,1)} %pad_select_fusion), channel_id=1, source_target_pairs={{0,8},{8,0},{16,24},{24,16},{1,9},{9,1},{17,25},{25,17},{2,10},{10... | collective-permute-start | bytes 2359304 | tf_op jit(solution)/shard_map/ppermute | solution.py:90
  315.6 27.4 %collective-permute-start.52 = (bf16[192,2048]{1,0:T(8,128)(2,1)}, bf16[192,2048]{1,0:T(8,128)(2,1)S(1)}, u32[]{:S(2)}, u32[]{:S(2)}) collective-permute-start(bf16[192,2048]{1,0:T(8,128)(2,1)} %get-tuple-element.124), channel_id=1, source_target_pairs={{2,4},{3,5},{4,2},{5,3},{10,12},{11,13},{12,10},{13,11},{18,20},{1... | collective-permute-start | bytes 2359304 | tf_op jit(solution)/shard_map/ppermute | solution.py:94
  321.4 51.0 %collective-permute-start.51 = (bf16[192,2048]{1,0:T(8,128)(2,1)S(1)}, bf16[192,2048]{1,0:T(8,128)(2,1)S(1)}, u32[]{:S(2)}, u32[]{:S(2)}) collective-permute-start(bf16[192,2048]{1,0:T(8,128)(2,1)S(1)} %dynamic-slice_add_fusion), channel_id=1, source_target_pairs={{0,4},{1,5},{4,0},{5,1},{2,6},{3,7},{6,2},{7,3},{8,12},{9,13},{12,... | collective-permute-start | bytes 2359304 | tf_op jit(solution)/shard_map/ppermute | solution.py:94
  323.8 64.4 %collective-permute-start.35 = (bf16[768,1280]{1,0:T(8,128)(2,1)S(1)}, bf16[768,1280]{1,0:T(8,128)(2,1)S(1)}, u32[]{:S(2)}, u32[]{:S(2)}) collective-permute-start(bf16[768,1280]{1,0:T(8,128)(2,1)S(1)} %copy-done.13), channel_id=1, source_target_pairs={{0,8},{8,0},{16,24},{24,16},{1,9},{9,1},{17,25},{25,17},{2,10},{10... | collective-permute-start | bytes 5898248 | tf_op jit(solution)/shard_map/ppermute | solution.py:90
  325.4 48.6 %collective-permute-start.43 = (bf16[4,96,512]{2,1,0:T(8,128)(2,1)S(1)}, bf16[4,96,512]{2,1,0:T(8,128)(2,1)S(1)}, u32[]{:S(2)}, u32[]{:S(2)}) collective-permute-start(bf16[4,96,512]{2,1,0:T(8,128)(2,1)S(1)} %dynamic-slice_bitcast_fusion.1), channel_id=1, source_target_pairs={{0,1},{1,0},{2,3},{3,2},{4,5},{5,4},{6,7},{7,6},{8,9},{9,8},{10,11... | collective-permute-start | bytes 1179656 | tf_op jit(solution)/shard_map/ppermute | solution.py:90
  339.5 52.1 %collective-permute-start.34 = (bf16[256,768]{1,0:T(8,128)(2,1)S(1)}, bf16[256,768]{1,0:T(8,128)(2,1)S(1)}, u32[]{:S(2)}, u32[]{:S(2)}) collective-permute-start(bf16[256,768]{1,0:T(8,128)(2,1)S(1)} %slice.101), channel_id=1, source_target_pairs={{0,16},{8,24},{16,0},{24,8},{1,17},{9,25},{17,1},{25,9},{2,18},{10... | collective-permute-start | bytes 1179656 | tf_op jit(solution)/shard_map/ppermute | solution.py:90
  (73 other events, 814.9 us)
